TPU v7x, 32 devices: a whole 2x2x4 slice. The times are simulated.
32 devices in a mesh: seq: 8 (over z, x), tp: 4 (over y, core).
Axes of the slice: x: 2, y: 2, z: 4, core: 2. Of those that a mesh axis runs over, the one named last changes fastest.
Arguments:
- query_heads: bfloat16 [2048, 2048], P('seq', 'tp'), may hold values from -96 to 96
- key_heads: bfloat16 [2048, 2048], P('seq', 'tp'), may hold values from -4 to 4
- value_heads: bfloat16 [2048, 2048], P('seq', 'tp'), may hold values from -6 to 6
- residual: bfloat16 [2048, 4096], P('seq'), may hold values from -64 to 64
- out_weight: bfloat16 [2048, 4096], P('tp'), may hold values from -0.125 to 0.125
- ln_gain: float32 [4096], replicated, may hold values from 0.1 to 1.9
- up_source: bfloat16 [4096, 4096], P(None, 'tp'), may hold values from -0.09375 to 0.09375
- down_source: bfloat16 [4096, 4096], P('tp'), may hold values from -0.09375 to 0.09375
- copy_gain: float32 [4096], P('tp'), may hold values from 0.3 to 3
- neuron_source: int32 [4096], P('tp'), may hold values from 0 to 4095, as said below
- cotangent: bfloat16 [2048, 4096], P('seq'), may hold values from -6 to 6
Outputs:
- encoded: float32 [2048, 4096], P(('seq', 'tp'))
- grad_query: float32 [2048, 2048], P('seq', 'tp')
- grad_key: float32 [2048, 2048], P('seq', 'tp')
- grad_value: float32 [2048, 2048], P('seq', 'tp')
- grad_residual: float32 [2048, 4096], P('seq', 'tp')
Inputs may be any that keep to these rules, and one draw needn't show every extreme that they name: Added neuron j splits a source neuron of its own group: neuron_source[j] // 1024 == j // 1024.
All inputs are finite; a program needn't handle non-finite values.
Results may differ from a plain program's by a relative error of at most 0.035.
Values may be sent and summed in bfloat16 or wider, within the bound.
A program may use at most 128 MiB of HBM per device.

v0:
```python
import functools
import math

import jax
import jax.numpy as jnp
from jax import lax
from jax.experimental import pallas as pl
from jax.experimental.pallas import tpu as pltpu
from jax.sharding import PartitionSpec as P

HEAD_DIM = 128
OFFSETS = (-2, -1, 1, 2)
CHUNKS = 4
TILE = 512
epsilon = 1e-05
MESH = pl.DeviceIdType.MESH
VM = pltpu.VMEM
F32 = jnp.float32
BF16 = jnp.bfloat16
SCALE = 1.0 / math.sqrt(HEAD_DIM)


def dot_nn(a, b):
    return jnp.dot(a, b, preferred_element_type=F32)


def dot_nt(a, b):
    return lax.dot_general(a, b, (((1,), (1,)), ((), ())), preferred_element_type=F32)


def dot_tn(a, b):
    return lax.dot_general(a, b, (((0,), (0,)), ((), ())), preferred_element_type=F32)


def remote(src, dst, send, recv, **where):
    return pltpu.make_async_remote_copy(
        src_ref=src, dst_ref=dst, send_sem=send, recv_sem=recv, device_id=where, device_id_type=MESH
    )


class Blocks:
    def __init__(self, count):
        self.count = count
        self.place = lax.axis_index("seq")

    def there(self, offset):
        other = self.place + offset
        return (other >= 0) & (other < self.count)

    def greet(self, barrier):
        for offset in OFFSETS:
            @pl.when(self.there(offset))
            def _():
                pl.semaphore_signal(
                    barrier, inc=1, device_id={"seq": self.place + offset}, device_id_type=MESH
                )

    def greeted(self, barrier, more=0):
        peers = sum(self.there(offset).astype(jnp.int32) for offset in OFFSETS)
        pl.semaphore_wait(barrier, peers + more)

    def copy(self, src, window, send, recv, to, slot, sent):
        return remote(src, window.at[slot], send.at[sent], recv.at[slot], seq=self.place + to)

    def send(self, src, window, send, recv):
        for index, offset in enumerate(OFFSETS):
            @pl.when(self.there(offset))
            def _():
                self.copy(src, window, send, recv, offset, 3 - index, index).start()

    def clear(self, window):
        for index, offset in enumerate(OFFSETS):
            @pl.when(jnp.logical_not(self.there(offset)))
            def _():
                window[index] = jnp.zeros(window.shape[1:], window.dtype)

    def arrive(self, src, window, send, recv, index):
        offset = OFFSETS[index]
        @pl.when(self.there(offset))
        def _():
            self.copy(src, window, send, recv, offset, index, index).wait_recv()

    def left(self, src, window, send, recv):
        for index, offset in enumerate(OFFSETS):
            @pl.when(self.there(offset))
            def _():
                self.copy(src, window, send, recv, offset, 3 - index, index).wait_send()


class Group:
    def __init__(self):
        me = lax.axis_index("tp")
        chip, core = lax.div(me, 2), lax.rem(me, 2)
        self.me = me
        self.sibling = chip * 2 + 1 - core
        self.far = (1 - chip) * 2 + core
        self.across = (1 - chip) * 2 + 1 - core

    def greet(self, barrier):
        for other in (self.sibling, self.far):
            pl.semaphore_signal(barrier, inc=1, device_id={"tp": other}, device_id_type=MESH)


def attend_kernel(
    count, q_ref, k_ref, v_ref, cot_ref, down_ref,
    out_ref, kwin, vwin, stat_ref, gm_ref,
    prob, cot_buf, down_buf, ks, kr, vs, vr, cot_sem, down_sem,
):
    blocks = Blocks(count)
    pieces, depth = down_buf.shape[:2]
    cot_copy = pltpu.make_async_copy(cot_ref, cot_buf, cot_sem)
    cot_copy.start()
    loads = [
        pltpu.make_async_copy(
            down_ref.at[pl.ds(i * depth, depth)], down_buf.at[i], down_sem.at[i]
        )
        for i in range(pieces)
    ]
    for load in loads:
        load.start()
    barrier = pltpu.get_barrier_semaphore()
    blocks.greet(barrier)
    blocks.greeted(barrier)
    blocks.send(k_ref, kwin, ks, kr)
    blocks.send(v_ref, vwin, vs, vr)
    blocks.clear(kwin)
    blocks.clear(vwin)
    rows, width = q_ref.shape
    heads = width // HEAD_DIM
    cot_copy.wait()
    for i in range(pieces):
        loads[i].wait()
        gm_ref[:, i * depth : (i + 1) * depth] = dot_nt(cot_buf[...], down_buf[i])
    for index in range(4):
        blocks.arrive(k_ref, kwin, ks, kr, index)
    bias = [jnp.where(blocks.there(offset), 0.0, -1e30).astype(F32) for offset in OFFSETS]
    lane = lax.broadcasted_iota(jnp.int32, (rows, 128), 1)
    stats = jnp.zeros((rows, 128), F32)
    for h in range(heads):
        cols = slice(h * HEAD_DIM, (h + 1) * HEAD_DIM)
        qh = q_ref[:, cols]
        scores = [dot_nt(qh, k_ref[:, cols]) * SCALE]
        for index in range(4):
            scores.append(dot_nt(qh, kwin[index, :, cols]) * SCALE + bias[index])
        top = scores[0]
        for s in scores[1:]:
            top = jnp.maximum(top, s)
        top = jnp.max(top, axis=1, keepdims=True)
        exps = [jnp.exp(s - top) for s in scores]
        total = exps[0]
        for e in exps[1:]:
            total = total + e
        inverse = 1.0 / jnp.sum(total, axis=1, keepdims=True)
        for index in range(5):
            prob[h, index] = (exps[index] * inverse).astype(BF16)
        stats = jnp.where(lane == h, top, stats)
        stats = jnp.where(lane == heads + h, inverse, stats)
    stat_ref[...] = jnp.transpose(stats)[: 2 * heads]
    for index in range(4):
        blocks.arrive(v_ref, vwin, vs, vr, index)
    for h in range(heads):
        cols = slice(h * HEAD_DIM, (h + 1) * HEAD_DIM)
        acc = dot_nn(prob[h, 0], v_ref[:, cols])
        for index in range(4):
            acc = acc + dot_nn(prob[h, index + 1], vwin[index, :, cols])
        out_ref[:, cols] = acc.astype(BF16)
    blocks.left(k_ref, kwin, ks, kr)
    blocks.left(v_ref, vwin, vs, vr)


def attend(count, q, k, v, cotangent, down):
    rows, width = q.shape
    src, model = down.shape
    pieces = 4
    heads = width // HEAD_DIM
    win = jax.ShapeDtypeStruct((4, rows, width), BF16)
    dma = pltpu.SemaphoreType.DMA((4,))
    return pl.pallas_call(
        functools.partial(attend_kernel, count),
        out_shape=(
            jax.ShapeDtypeStruct((rows, width), BF16),
            win,
            win,
            jax.ShapeDtypeStruct((2 * heads, rows), F32),
            jax.ShapeDtypeStruct((rows, src), F32),
        ),
        in_specs=[pl.BlockSpec(memory_space=VM)] * 3 + [pl.BlockSpec(memory_space=pl.ANY)] * 2,
        out_specs=(pl.BlockSpec(memory_space=VM),) * 5,
        scratch_shapes=[
            VM((heads, 5, rows, rows), BF16),
            VM(cotangent.shape, BF16),
            VM((pieces, src // pieces, model), BF16),
            dma, dma, dma, dma,
            pltpu.SemaphoreType.DMA(()),
            pltpu.SemaphoreType.DMA((pieces,)),
        ],
        compiler_params=pltpu.CompilerParams(
            collective_id=1, has_side_effects=True, vmem_limit_bytes=48 << 20
        ),
        name="attend",
    )(q, k, v, cotangent, down)


def reduce_first(group, own, part, mine, sbuf1, rbuf1, s1, r1):
    part((group.across, group.sibling), sbuf1)
    copies = [
        remote(sbuf1.at[i], rbuf1.at[i], s1.at[i], r1.at[i], tp=group.sibling) for i in range(2)
    ]
    for copy in copies:
        copy.start()
    part((group.far, group.me), mine)
    return copies


def reduce_second(group, own, mine, rbuf1, sbuf2, rbuf2, s2, r2, copies):
    copies[0].wait_recv()
    rows = own // CHUNKS
    out = []
    for ch in range(CHUNKS):
        sl = slice(ch * rows, (ch + 1) * rows)
        sbuf2[ch] = (mine[0, sl].astype(F32) + rbuf1[0, sl].astype(F32)).astype(BF16)
        copy = remote(sbuf2.at[ch], rbuf2.at[ch], s2.at[ch], r2.at[ch], tp=group.far)
        copy.start()
        out.append(copy)
    copies[1].wait_recv()
    return out


def spread(group, own, full, finish, seconds, ags, agr):
    rows = own // CHUNKS

    def at(owner, ch):
        return full.at[pl.ds(pl.multiple_of(owner * own + ch * rows, rows), rows)]

    to_sib, to_far, passed = [], [], []
    for ch in range(CHUNKS):
        seconds[ch].wait_recv()
        finish(ch, at(group.me, ch))
        mine = at(group.me, ch)
        to_far.append(remote(mine, mine, ags.at[ch, 0], agr.at[ch, 0], tp=group.far))
        to_far[ch].start()
        to_sib.append(remote(mine, mine, ags.at[ch, 1], agr.at[ch, 1], tp=group.sibling))
        to_sib[ch].start()
    for ch in range(CHUNKS):
        to_far[ch].wait_recv()
        got = at(group.far, ch)
        passed.append(remote(got, got, ags.at[ch, 2], agr.at[ch, 2], tp=group.sibling))
        passed[ch].start()
    for ch in range(CHUNKS):
        to_sib[ch].wait_recv()
        passed[ch].wait_recv()
    return to_sib + to_far + passed


def norm_kernel(
    count, att_ref, w_ref, res_ref, gain_ref, q_ref, stat_ref,
    up_ref, pick_ref, gm_ref, inv_ref, cg_ref,
    merged_ref, gh_ref, unit_ref, sigma_ref, qwin, swin,
    mine, sbuf1, rbuf1, sbuf2, rbuf2, res_buf, full, up_buf,
    s1, r1, s2, r2, ags, agr, qs, qr, ss, sr, res_sem, up_sem,
):
    blocks, group = Blocks(count), Group()
    own, width = unit_ref.shape
    rows = own // CHUNKS
    fetch = pltpu.make_async_copy(
        res_ref.at[pl.ds(pl.multiple_of(group.me * own, own), own)], res_buf, res_sem
    )
    fetch.start()
    up_load = pltpu.make_async_copy(up_ref, up_buf, up_sem)
    up_load.start()
    barrier = pltpu.get_barrier_semaphore()
    group.greet(barrier)
    blocks.greet(barrier)
    blocks.greeted(barrier, 2)
    blocks.send(q_ref, qwin, qs, qr)
    blocks.send(stat_ref, swin, ss, sr)

    def part(owners, dst):
        lhs = jnp.concatenate(
            [att_ref[pl.ds(pl.multiple_of(o * own, own), own), :] for o in owners], axis=0
        )

        @pl.loop(0, width // TILE)
        def _(ct):
            cols = pl.ds(pl.multiple_of(ct * TILE, TILE), TILE)
            r = dot_nn(lhs, w_ref[:, cols]).astype(BF16)
            dst[0, :, cols] = r[:own]
            dst[1, :, cols] = r[own:]

    firsts = reduce_first(group, own, part, mine, sbuf1, rbuf1, s1, r1)
    blocks.clear(qwin)
    blocks.clear(swin)
    seconds = reduce_second(group, own, mine, rbuf1, sbuf2, rbuf2, s2, r2, firsts)
    fetch.wait()

    def finish(ch, dst):
        sl = slice(ch * rows, (ch + 1) * rows)
        stream = (
            res_buf[sl].astype(F32)
            + mine[1, sl].astype(F32)
            + rbuf1[1, sl].astype(F32)
            + rbuf2[ch].astype(F32)
        )
        centered = stream - jnp.mean(stream, axis=1, keepdims=True)
        sigma = jnp.sqrt(jnp.mean(centered * centered, axis=1, keepdims=True) + epsilon)
        unit = centered / sigma
        unit_ref[sl] = unit
        sigma_ref[sl] = jnp.broadcast_to(sigma, (rows, 128))
        dst[...] = (unit * gain_ref[...]).astype(BF16)

    tails = spread(group, own, full, finish, seconds, ags, agr)
    up_load.wait()
    half = 2 * own

    @pl.loop(0, full.shape[0] // half)
    def _(b):
        span = pl.ds(pl.multiple_of(b * half, half), half)
        hidden = dot_nn(full[span, :], up_buf[...])
        copies = dot_nn(hidden.astype(BF16), pick_ref[...]) * cg_ref[...]
        act_src, slope_src = gelu_slope(hidden)
        act_copy, slope_copy = gelu_slope(copies)
        summed = act_src + dot_nt(act_copy.astype(BF16), pick_ref[...])
        merged_ref[span, :] = (summed * inv_ref[...]).astype(BF16)
        scaled = gm_ref[span, :] * inv_ref[...]
        grad_copy = dot_nn(scaled.astype(BF16), pick_ref[...]) * slope_copy * cg_ref[...]
        gh_ref[span, :] = (
            scaled * slope_src + dot_nt(grad_copy.astype(BF16), pick_ref[...])
        ).astype(BF16)

    for copy in firsts + seconds + tails:
        copy.wait_send()
    for index in range(4):
        blocks.arrive(q_ref, qwin, qs, qr, index)
        blocks.arrive(stat_ref, swin, ss, sr, index)
    blocks.left(q_ref, qwin, qs, qr)
    blocks.left(stat_ref, swin, ss, sr)


def reduce_scratch(own, width):
    two = VM((2, own, width), BF16)
    chunk = VM((CHUNKS, own // CHUNKS, width), BF16)
    return [two, two, two, chunk, chunk]


def reduce_sems():
    dma = pltpu.SemaphoreType.DMA
    return [dma((2,)), dma((2,)), dma((CHUNKS,)), dma((CHUNKS,))]


def norm_stage(count, groups, att, w, residual, gain, q, stats, up, pick, gm, inverse, copy_gain):
    tok, width = residual.shape
    own = tok // groups
    dma = pltpu.SemaphoreType.DMA
    vm = pl.BlockSpec(memory_space=VM)
    far = pl.BlockSpec(memory_space=pl.ANY)
    return pl.pallas_call(
        functools.partial(norm_kernel, count),
        out_shape=(
            jax.ShapeDtypeStruct(gm.shape, BF16),
            jax.ShapeDtypeStruct(gm.shape, BF16),
            jax.ShapeDtypeStruct((own, width), F32),
            jax.ShapeDtypeStruct((own, 128), F32),
            jax.ShapeDtypeStruct((4,) + q.shape, BF16),
            jax.ShapeDtypeStruct((4,) + stats.shape, F32),
        ),
        in_specs=[vm, vm, far, vm, vm, vm, far, vm, vm, vm, vm],
        out_specs=(vm,) * 6,
        scratch_shapes=reduce_scratch(own, width)
        + [VM((own, width), BF16), VM((tok, width), BF16), VM(up.shape, BF16)]
        + reduce_sems()
        + [dma((CHUNKS, 3)), dma((CHUNKS, 3))]
        + [dma((4,))] * 4
        + [dma(())] * 2,
        compiler_params=pltpu.CompilerParams(
            collective_id=2, has_side_effects=True, vmem_limit_bytes=48 << 20
        ),
        name="norm_stage",
    )(att, w, residual, gain, q, stats, up, pick, gm, inverse, copy_gain)


def back_kernel(
    gh_ref, up_ref, merged_ref, down_ref, cot_ref, gain_ref, unit_ref, sigma_ref,
    full, ffn_ref,
    mine, sbuf1, rbuf1, sbuf2, rbuf2, cot_buf, w_ref, down_buf,
    s1, r1, s2, r2, ags, agr, cot_sem, up_sem, down_sem,
):
    group = Group()
    own, width = unit_ref.shape
    rows = own // CHUNKS
    tiles = width // TILE

    def up_load(ct):
        span = pl.ds(pl.multiple_of(ct * TILE, TILE), TILE)
        return pltpu.make_async_copy(up_ref.at[span], w_ref.at[span], up_sem.at[ct])

    def down_load(ct):
        span = pl.ds(pl.multiple_of(ct * TILE, TILE), TILE)
        return pltpu.make_async_copy(down_ref.at[:, span], down_buf.at[ct], down_sem.at[ct])

    for ct in range(tiles):
        up_load(ct).start()
    fetch = pltpu.make_async_copy(
        cot_ref.at[pl.ds(pl.multiple_of(group.me * own, own), own)], cot_buf, cot_sem
    )
    fetch.start()
    barrier = pltpu.get_barrier_semaphore()
    group.greet(barrier)
    pl.semaphore_wait(barrier, 2)

    def part(owners, dst):
        lhs = jnp.concatenate(
            [gh_ref[pl.ds(pl.multiple_of(o * own, own), own), :] for o in owners], axis=0
        )

        @pl.loop(0, tiles)
        def _(ct):
            if dst is sbuf1:
                up_load(ct).wait()
            cols = pl.ds(pl.multiple_of(ct * TILE, TILE), TILE)
            r = dot_nt(lhs, w_ref[cols, :]).astype(BF16)
            dst[0, :, cols] = r[:own]
            dst[1, :, cols] = r[own:]

    for ct in range(tiles):
        down_load(ct).start()
    firsts = reduce_first(group, own, part, mine, sbuf1, rbuf1, s1, r1)
    seconds = reduce_second(group, own, mine, rbuf1, sbuf2, rbuf2, s2, r2, firsts)
    fetch.wait()

    @pl.loop(0, tiles)
    def _(ct):
        down_load(ct).wait()
        cols = pl.ds(pl.multiple_of(ct * TILE, TILE), TILE)
        ffn_ref[:, cols] = dot_nn(merged_ref[...], down_buf[ct]).astype(BF16)

    def finish(ch, dst):
        sl = slice(ch * rows, (ch + 1) * rows)
        grad = (
            cot_buf[sl].astype(F32)
            + mine[1, sl].astype(F32)
            + rbuf1[1, sl].astype(F32)
            + rbuf2[ch].astype(F32)
        )
        scaled = grad * gain_ref[...]
        unit = unit_ref[sl]
        mean = jnp.mean(scaled, axis=1, keepdims=True)
        along = jnp.mean(scaled * unit, axis=1, keepdims=True)
        dst[...] = ((scaled - mean - unit * along) / sigma_ref[sl, :1]).astype(BF16)

    tails = spread(group, own, full, finish, seconds, ags, agr)
    for copy in firsts + seconds + tails:
        copy.wait_send()


def back_stage(groups, gh, up, merged, down, cotangent, gain, unit, sigma):
    tok, width = cotangent.shape
    own = tok // groups
    dma = pltpu.SemaphoreType.DMA
    vm = pl.BlockSpec(memory_space=VM)
    far = pl.BlockSpec(memory_space=pl.ANY)
    tiles = width // TILE
    return pl.pallas_call(
        back_kernel,
        out_shape=(jax.ShapeDtypeStruct((tok, width), BF16),) * 2,
        in_specs=[vm, far, vm, far, far, vm, vm, vm],
        out_specs=(vm, vm),
        scratch_shapes=reduce_scratch(own, width)
        + [VM((own, width), BF16), VM(up.shape, BF16), VM((tiles, down.shape[0], TILE), BF16)]
        + reduce_sems()
        + [dma((CHUNKS, 3)), dma((CHUNKS, 3)), dma(()), dma((tiles,)), dma((tiles,))],
        compiler_params=pltpu.CompilerParams(
            collective_id=3, has_side_effects=True, vmem_limit_bytes=48 << 20
        ),
        name="back_stage",
    )(gh, up, merged, down, cotangent, gain, unit, sigma)


def grads_kernel(
    count, low_ref, w_ref, att_ref, q_ref, k_ref, v_ref, kwin, vwin, qwin, stat_ref, swin,
    ffn_ref, unit_ref, gain_ref,
    enc_ref, gq_ref, gk_ref, gv_ref,
    dwin, twin, do_ref, delta_ref, rbuf1, sbuf2, rbuf2,
    ds_, dr, ts, tr, s1, r1, s2, r2,
):
    blocks, group = Blocks(count), Group()
    own, width = unit_ref.shape
    tok, cols_all = q_ref.shape
    heads = cols_all // HEAD_DIM
    rows = own // CHUNKS
    barrier = pltpu.get_barrier_semaphore()
    group.greet(barrier)
    blocks.greet(barrier)
    blocks.greeted(barrier, 2)

    def ffn_rows(owner):
        return ffn_ref.at[pl.ds(pl.multiple_of(owner * own, own), own)]

    firsts = [
        remote(ffn_rows(owner), rbuf1.at[i], s1.at[i], r1.at[i], tp=group.sibling)
        for i, owner in enumerate((group.across, group.sibling))
    ]
    for copy in firsts:
        copy.start()
    lane = lax.broadcasted_iota(jnp.int32, (tok, 128), 1)
    grad_att = dot_nt(low_ref[...], w_ref[...]).astype(BF16)
    do_ref[...] = grad_att
    blocks.send(do_ref, dwin, ds_, dr)
    deltas = jnp.zeros((tok, 128), F32)
    for h in range(heads):
        cols = slice(h * HEAD_DIM, (h + 1) * HEAD_DIM)
        delta = jnp.sum(
            grad_att[:, cols].astype(F32) * att_ref[:, cols].astype(F32), axis=1, keepdims=True
        )
        deltas = jnp.where(lane == h, delta, deltas)
    delta_ref[...] = jnp.transpose(deltas)[:8]
    blocks.send(delta_ref, twin, ts, tr)
    blocks.clear(dwin)
    blocks.clear(twin)
    firsts[0].wait_recv()
    seconds = []
    far_rows = ffn_rows(group.far)
    for ch in range(CHUNKS):
        sl = slice(ch * rows, (ch + 1) * rows)
        sbuf2[ch] = (far_rows[sl].astype(F32) + rbuf1[0, sl].astype(F32)).astype(BF16)
        seconds.append(remote(sbuf2.at[ch], rbuf2.at[ch], s2.at[ch], r2.at[ch], tp=group.far))
        seconds[ch].start()

    def pair(queries, keys, values, grads, stats, delta_row, h):
        top = stats[pl.ds(h, 1), :]
        inverse = stats[pl.ds(heads + h, 1), :]
        prob = jnp.exp(dot_nt(keys, queries) * SCALE - top) * inverse
        slope = (prob * (dot_nt(values, grads) - delta_row[pl.ds(h, 1), :])).astype(BF16)
        return prob.astype(BF16), slope

    @pl.loop(0, heads)
    def _(h):
        cols = pl.ds(pl.multiple_of(h * HEAD_DIM, HEAD_DIM), HEAD_DIM)
        qh, gh = q_ref[:, cols], do_ref[:, cols]
        kh, vh = k_ref[:, cols], v_ref[:, cols]
        prob, slope = pair(qh, kh, vh, gh, stat_ref, delta_ref, h)
        gv_ref[:, cols] = dot_nn(prob, gh)
        gk_ref[:, cols] = dot_nn(slope, qh)
        acc = dot_tn(slope, kh)
        for index in range(4):
            k_off, v_off = kwin[index, :, cols], vwin[index, :, cols]
            live = jnp.where(blocks.there(OFFSETS[index]), 1.0, 0.0).astype(F32)
            _, slope = pair_off(qh, k_off, v_off, gh, stat_ref, delta_ref, h, live)
            acc = acc + dot_tn(slope, k_off)
        gq_ref[:, cols] = acc * SCALE

    for index in range(4):
        blocks.arrive(do_ref, dwin, ds_, dr, index)
        blocks.arrive(delta_ref, twin, ts, tr, index)

        @pl.when(blocks.there(OFFSETS[index]))
        def _():
            @pl.loop(0, heads)
            def _(h):
                cols = pl.ds(pl.multiple_of(h * HEAD_DIM, HEAD_DIM), HEAD_DIM)
                kh, vh = k_ref[:, cols], v_ref[:, cols]
                q_off, g_off = qwin[index, :, cols], dwin[index, :, cols]
                prob, slope = pair(q_off, kh, vh, g_off, swin.at[index], twin.at[index], h)
                gv_ref[:, cols] += dot_nn(prob, g_off)
                gk_ref[:, cols] += dot_nn(slope, q_off)

    gk_ref[...] = gk_ref[...] * SCALE

    firsts[1].wait_recv()
    near_rows = ffn_rows(group.me)
    for ch in range(CHUNKS):
        sl = slice(ch * rows, (ch + 1) * rows)
        seconds[ch].wait_recv()
        enc_ref[sl] = unit_ref[sl] * gain_ref[...] + (
            near_rows[sl].astype(F32) + rbuf1[1, sl].astype(F32) + rbuf2[ch].astype(F32)
        )
    for copy in firsts + seconds:
        copy.wait_send()
    blocks.left(do_ref, dwin, ds_, dr)
    blocks.left(delta_ref, twin, ts, tr)


def pair_off(queries, keys, values, grads, stats, delta_row, h, live):
    heads = stats.shape[0] // 2
    bias = (live - 1.0) * 1e30
    prob = jnp.exp(dot_nt(keys, queries) * SCALE + bias - stats[pl.ds(h, 1), :])
    prob = prob * stats[pl.ds(heads + h, 1), :]
    slope = (prob * (dot_nt(values, grads) - delta_row[pl.ds(h, 1), :])).astype(BF16)
    return None, slope


def grads_stage(count, low, w, att, q, k, v, kwin, vwin, qwin, stats, swin, ffn, unit, gain):
    tok, width = low.shape
    own = unit.shape[0]
    dma = pltpu.SemaphoreType.DMA
    vm = pl.BlockSpec(memory_space=VM)
    chunk = VM((CHUNKS, own // CHUNKS, width), BF16)
    grad = jax.ShapeDtypeStruct(q.shape, F32)
    return pl.pallas_call(
        functools.partial(grads_kernel, count),
        out_shape=(jax.ShapeDtypeStruct((own, width), F32), grad, grad, grad),
        in_specs=[vm] * 14,
        out_specs=(vm,) * 4,
        scratch_shapes=[
            VM((4,) + q.shape, BF16),
            VM((4, 8, tok), F32),
            VM(q.shape, BF16),
            VM((8, tok), F32),
            VM((2, own, width), BF16),
            chunk,
            chunk,
        ]
        + [dma((4,))] * 4
        + reduce_sems(),
        compiler_params=pltpu.CompilerParams(
            collective_id=4, has_side_effects=True, vmem_limit_bytes=48 << 20
        ),
        name="grads_stage",
    )(low, w, att, q, k, v, kwin, vwin, qwin, stats, swin, ffn, unit, gain)


def gelu_slope(v):
    rate = math.sqrt(2.0 / math.pi)
    square = v * v
    bend = jnp.tanh(rate * v * (1.0 + 0.044715 * square))
    level = 0.5 * (1.0 + bend)
    slope = level + (0.5 * rate) * v * (1.0 - bend * bend) * (1.0 + 0.134145 * square)
    return v * level, slope


def shards(
    count,
    groups,
    query_heads,
    key_heads,
    value_heads,
    residual,
    out_weight,
    ln_gain,
    up_source,
    down_source,
    copy_gain,
    neuron_source,
    cotangent,
):
    model_width = residual.shape[1]
    tp_place = lax.axis_index("tp")
    gain = ln_gain[None, :]
    src_width = up_source.shape[1]
    local_source = neuron_source - tp_place * src_width
    pick = (
        lax.broadcasted_iota(jnp.int32, (src_width, local_source.shape[0]), 0)
        == local_source[None, :]
    )
    counts = 1.0 + jnp.sum(pick.astype(F32), axis=1)
    inverse = 1.0 / counts
    pick = pick.astype(BF16)

    attended, kwin, vwin, stats, grad_merged = attend(
        count, query_heads, key_heads, value_heads, cotangent, down_source
    )
    merged, grad_hidden, unit, sigma, qwin, swin = norm_stage(
        count, groups, attended, out_weight, residual, gain, query_heads, stats,
        up_source, pick, grad_merged, inverse[None, :], copy_gain[None, :],
    )
    grad_low, ffn_part = back_stage(
        groups, grad_hidden, up_source, merged, down_source, cotangent, gain, unit, sigma
    )
    encoded, grad_query, grad_key, grad_value = grads_stage(
        count, grad_low, out_weight, attended, query_heads, key_heads, value_heads,
        kwin, vwin, qwin, stats, swin, ffn_part, unit, gain,
    )
    col_width = model_width // groups
    grad_residual = lax.dynamic_slice_in_dim(grad_low, tp_place * col_width, col_width, 1)
    return (encoded, grad_query, grad_key, grad_value, grad_residual.astype(F32))


def solution(mesh):
    in_specs = (
        P("seq", "tp"),
        P("seq", "tp"),
        P("seq", "tp"),
        P("seq", None),
        P("tp", None),
        P(),
        P(None, "tp"),
        P("tp", None),
        P("tp"),
        P("tp"),
        P("seq", None),
    )
    out_specs = (
        P(("seq", "tp"), None),
        P("seq", "tp"),
        P("seq", "tp"),
        P("seq", "tp"),
        P("seq", "tp"),
    )
    body = functools.partial(shards, mesh.shape["seq"], mesh.shape["tp"])
    return jax.shard_map(body, mesh=mesh, in_specs=in_specs, out_specs=out_specs, check_vma=False)
```

profile of v0, /device:TPU:0, one launch (start us, length us, event | category | flops | bytes accessed | tf_op | source)
XLA Modules:
  0.0 142.7 jit_solution(17798942214914166388)
XLA Ops:
  0.6 0.7 broadcast_subtract_fusion
  1.3 0.5 convert_reduce_fusion
  1.8 2.2 %fusion.pick_ref = bf16[1024,1024]{1,0:T(8,128)(2,1)} fusion(s32[1024]{0:T(1024)S(1)} %broadcast_subtract_fusion), kind=kLoop, calls=%fused_computation.2 | loop fusion | flops 2097152 | bytes 2101248 | tf_op jit(solution)/shard_map/convert_element_type | solution.py:656
  4.1 0.0 copy-start.2
  4.1 0.9 copy-done.2
  5.0 0.0 copy-start.5
  5.0 0.9 copy-done.5
  6.0 0.0 copy-start.7
  6.0 0.9 copy-done.7
  6.9 0.0 copy-start.9
  6.9 0.0 copy-start.10
  6.9 24.1 %attend.1 = (bf16[256,512]{1,0:T(8,128)(2,1)S(1)}, bf16[4,256,512]{2,1,0:T(8,128)(2,1)S(1)}, bf16[4,256,512]{2,1,0:T(8,128)(2,1)S(1)}, f32[8,256]{1,0:T(8,128)S(1)}, f32[256,1024]{1,0:T(8,128)S(1)}) custom-call(bf16[256,512]{1,0:T(8,128)(2,1)S(1)} %copy-done.2, bf16[256,512]{1,0:T(8,128)(2,1)S(1)} %copy-done.5, bf16[256,512]{1,0:T(8,128)(2,1)S(1)} %copy-done.7, ...), custom_call_target="tpu_custom_call" | custom-call | tf_op jit(solution)/shard_map/attend/pallas_call | solution.py:178
  31.0 0.0 copy-done.9
  31.0 0.0 copy-done.10
  31.0 44.7 %norm_stage.1 = (bf16[256,1024]{1,0:T(8,128)(2,1)S(1)}, bf16[256,1024]{1,0:T(8,128)(2,1)S(1)}, f32[64,4096]{1,0:T(8,128)S(1)}, f32[64,128]{1,0:T(8,128)S(1)}, bf...) custom-call(bf16[256,512]{1,0:T(8,128)(2,1)S(1)} %get-tuple-element.22.att_ref, bf16[512,4096]{1,0:T(8,128)(2,1)} %w_ref.3, ...), custom_call_target="tpu_custom_call" | custom-call | tf_op jit(solution)/shard_map/norm_stage/pallas_call | solution.py:356
  75.8 0.0 copy-start.4
  75.8 1.0 copy-done.4
  76.7 0.0 copy-start
  76.7 0.0 copy-start.3
  76.7 0.0 copy-start.6
  76.7 0.0 copy-start.8
  76.7 36.4 %back_stage.1 = (bf16[256,4096]{1,0:T(8,128)(2,1)S(1)}, bf16[256,4096]{1,0:T(8,128)(2,1)}) custom-call(bf16[256,1024]{1,0:T(8,128)(2,1)S(1)} %get-tuple-element.25.gh_ref, bf16[4096,1024]{1,0:T(8,128)(2,1)} %up_ref.3, bf16[256,1024]{1,0:T(8,128)(2,1)S(1)} %get-tuple-element.26.merged_ref, bf16[1024,4096]{1,0:T(8,128)(2,1)} %down_ref.3, ...), custom_call_target="tpu_custom_call" | custom-call | tf_op jit(solution)/shard_map/back_stage/pallas_call | solution.py:462
  113.2 0.0 copy-done
  113.2 0.0 copy-start.1
  113.2 1.3 copy-done.1
  114.5 0.0 copy-done.3
  114.5 0.0 copy-done.6
  114.5 0.0 copy-done.8
  114.5 22.7 %grads_stage.1 = (f32[64,4096]{1,0:T(8,128)S(1)}, f32[256,512]{1,0:T(8,128)S(1)}, f32[256,512]{1,0:T(8,128)S(1)}, f32[256,512]{1,0:T(8,128)S(1)}) custom-call(bf16[256,4096]{1,0:T(8,128)(2,1)} %copy-done.1, bf16[512,4096]{1,0:T(8,128)(2,1)} %w_ref.3, bf16[256,512]{1,0:T(8,128)(2,1)S(1)} %get-tuple-element.22.att_ref, bf16[256,512]{1,0:T(8,128)(2,1)S(1)} %copy-done.3, ...), custom_call_target="tpu_custom_call" | custom-call | tf_op jit(solution)/shard_map/grads_stage/pallas_call | solution.py:598
  137.2 2.1 %dynamic-slice_convert_fusion = f32[256,1024]{1,0:T(8,128)} fusion(bf16[256,4096]{1,0:T(8,128)(2,1)} %copy-done.1, s32[]{:T(128)S(6)} %select_n.3), kind=kLoop, calls=%fused_computation.3 | loop fusion | flops 262144 | bytes 1572868 | tf_op jit(solution)/shard_map/convert_element_type | solution.py:674
  139.4 1.0 copy.20
  140.3 0.8 copy.21
  141.1 0.8 copy.22
  141.9 0.8 copy.23
  (1 shorter events, 0.0 us)
Async XLA Ops:
  4.1 0.9 copy-start.2
  5.0 0.9 copy-start.5
  6.0 0.9 copy-start.7
  6.9 24.1 %copy-start.9 = (f32[4096]{0:T(1024)S(1)}, f32[4096]{0:T(1024)}, u32[]{:S(2)}) copy-start(f32[4096]{0:T(1024)} %param.16) | copy-start | bytes 49156
  6.9 24.1 %copy-start.10 = (f32[1024]{0:T(1024)S(1)}, f32[1024]{0:T(1024)}, u32[]{:S(2)}) copy-start(f32[1024]{0:T(1024)} %param.19) | copy-start | bytes 12292
  75.8 1.0 copy-start.4
  76.7 36.4 %copy-start = (f32[64,4096]{1,0:T(8,128)}, f32[64,4096]{1,0:T(8,128)S(1)}, u32[]{:S(2)}) copy-start(f32[64,4096]{1,0:T(8,128)S(1)} %get-tuple-element.27.unit_ref) | copy-start | bytes 3145732
  76.7 37.8 %copy-start.3 = (bf16[256,512]{1,0:T(8,128)(2,1)S(1)}, bf16[256,512]{1,0:T(8,128)(2,1)}, u32[]{:S(2)}) copy-start(bf16[256,512]{1,0:T(8,128)(2,1)} %q_ref.5) | copy-start | bytes 786436
  76.7 37.8 %copy-start.6 = (bf16[256,512]{1,0:T(8,128)(2,1)S(1)}, bf16[256,512]{1,0:T(8,128)(2,1)}, u32[]{:S(2)}) copy-start(bf16[256,512]{1,0:T(8,128)(2,1)} %k_ref.3) | copy-start | bytes 786436
  76.7 37.8 %copy-start.8 = (bf16[256,512]{1,0:T(8,128)(2,1)S(1)}, bf16[256,512]{1,0:T(8,128)(2,1)}, u32[]{:S(2)}) copy-start(bf16[256,512]{1,0:T(8,128)(2,1)} %v_ref.3) | copy-start | bytes 786436
  113.2 1.3 copy-start.1
where the time goes:
time: 145 us; the launch traced here: 143 us
  Pallas kernels  128 us (88%)
  local copies, waits for them, and re-layouts  8.49 us (6%)
  other arithmetic  5.55 us (4%)
    pallas_call x1, Pallas kernels, norm_stage(): pl.pallas_call(functools.partial(norm_kernel, count), out_shape=(jax.Shap...  44.7 us
    pallas_call x1, Pallas kernels, back_stage(): pl.pallas_call(back_kernel, out_shape=(jax.ShapeDtypeStruct((tok, width),...  36.4 us
    pallas_call x1, Pallas kernels, attend(): pl.pallas_call(functools.partial(attend_kernel, count), out_shape=(jax.Sh...  24.1 us
    pallas_call x1, Pallas kernels, grads_stage(): pl.pallas_call(functools.partial(grads_kernel, count), out_shape=(jax.Sha...  22.7 us
    unnamed x26, local copies, waits for them, and re-layouts  8.49 us

commit v1 on v0

v1 whole, which is shorter than its diff:
```python
import functools
import math

import jax
import jax.numpy as jnp
from jax import lax
from jax.experimental import pallas as pl
from jax.experimental.pallas import tpu as pltpu
from jax.sharding import PartitionSpec as P

HEAD_DIM = 128
OFFSETS = (-2, -1, 1, 2)
OWN = 4
HALVES = 2
PIECES = 4
TILE = 512
epsilon = 1e-05
MESH = pl.DeviceIdType.MESH
VM = pltpu.VMEM
F32 = jnp.float32
BF16 = jnp.bfloat16
SCALE = 1.0 / math.sqrt(HEAD_DIM)


def dot_nn(a, b):
    return jnp.dot(a, b, preferred_element_type=F32)


def dot_nt(a, b):
    return lax.dot_general(a, b, (((1,), (1,)), ((), ())), preferred_element_type=F32)


def dot_tn(a, b):
    return lax.dot_general(a, b, (((0,), (0,)), ((), ())), preferred_element_type=F32)


def remote(src, dst, send, recv, **where):
    return pltpu.make_async_remote_copy(
        src_ref=src, dst_ref=dst, send_sem=send, recv_sem=recv, device_id=where, device_id_type=MESH
    )


def gelu_slope(v):
    rate = math.sqrt(2.0 / math.pi)
    square = v * v
    bend = jnp.tanh(rate * v * (1.0 + 0.044715 * square))
    level = 0.5 * (1.0 + bend)
    slope = level + (0.5 * rate) * v * (1.0 - bend * bend) * (1.0 + 0.134145 * square)
    return v * level, slope


class Blocks:
    def __init__(self, count):
        self.count = count
        self.place = lax.axis_index("seq")
        self.even = lax.rem(self.place, 2) == 0

    def there(self, offset):
        other = self.place + offset
        return (other >= 0) & (other < self.count)

    def greet(self, barrier):
        for offset in OFFSETS:
            @pl.when(self.there(offset))
            def _():
                pl.semaphore_signal(
                    barrier, inc=1, device_id={"seq": self.place + offset}, device_id_type=MESH
                )

    def greeted(self, barrier, more):
        peers = sum(self.there(offset).astype(jnp.int32) for offset in OFFSETS)
        pl.semaphore_wait(barrier, peers + more)

    def copy(self, src, window, send, recv, index, slot):
        return remote(
            src, window(slot), send.at[index], recv.at[slot], seq=self.place + OFFSETS[index]
        )

    def send(self, src, window, send, recv):
        for index, offset in enumerate(OFFSETS):
            @pl.when(self.there(offset))
            def _():
                self.copy(src, window, send, recv, index, 3 - index).start()

    def arrive(self, src, window, send, recv):
        for index, offset in enumerate(OFFSETS):
            @pl.when(self.there(offset))
            def _():
                self.copy(src, window, send, recv, index, index).wait_recv()

    def left(self, src, window, send, recv):
        for index, offset in enumerate(OFFSETS):
            @pl.when(self.there(offset))
            def _():
                self.copy(src, window, send, recv, index, 3 - index).wait_send()

    def clear(self, window):
        for index, offset in enumerate(OFFSETS):
            @pl.when(jnp.logical_not(self.there(offset)))
            def _():
                ref = window(index)
                ref[...] = jnp.zeros(ref.shape, ref.dtype)


class Halo:
    def __init__(self, blocks, buf, send, recv, fwd, across):
        self.blocks, self.buf, self.send_sem, self.recv_sem, self.fwd = blocks, buf, send, recv, fwd
        self.across = across

    def window(self, slot):
        return self.buf.at[slot]

    def hops(self, even):
        return (0, 2 if even else 1, 3)

    def both(self, act):
        for even in (True, False):
            @pl.when(self.blocks.even == even)
            def _():
                act(even)

    def copy(self, index, slot):
        return self.blocks.copy(
            self.buf.at[OWN], self.window, self.send_sem, self.recv_sem, index, slot
        )

    def start(self):
        def act(even):
            for index in self.hops(even):
                @pl.when(self.blocks.there(OFFSETS[index]))
                def _():
                    self.copy(index, 3 - index).start()

        self.both(act)

    def passing(self, even):
        if self.across:
            return (3, 1, 2, 2) if even else (0, -1, 1, -2)
        return (2, 2, 1, 2) if even else (1, -2, 2, -2)

    def pass_copy(self, even):
        slot, to, there, need = self.passing(even)
        return remote(
            self.buf.at[slot], self.buf.at[there], self.fwd, self.recv_sem.at[there],
            seq=self.blocks.place + to,
        ), need

    def relay(self):
        def act(even):
            slot = self.passing(even)[0]
            copy, need = self.pass_copy(even)

            @pl.when(self.blocks.there(OFFSETS[slot]))
            def _():
                self.copy(slot, slot).wait_recv()

            @pl.when(self.blocks.there(need))
            def _():
                copy.start()

        self.both(act)

    def arrive(self):
        def act(even):
            for index in range(4):
                if index != self.passing(even)[0]:
                    @pl.when(self.blocks.there(OFFSETS[index]))
                    def _():
                        self.copy(index, index).wait_recv()

        self.both(act)

    def left(self):
        def act(even):
            for index in self.hops(even):
                @pl.when(self.blocks.there(OFFSETS[index]))
                def _():
                    self.copy(index, 3 - index).wait_send()
            copy, need = self.pass_copy(even)

            @pl.when(self.blocks.there(need))
            def _():
                copy.wait_send()

        self.both(act)


class Group:
    def __init__(self):
        me = lax.axis_index("tp")
        chip, core = lax.div(me, 2), lax.rem(me, 2)
        self.me = me
        self.sibling = chip * 2 + 1 - core
        self.far = (1 - chip) * 2 + core
        self.across = (1 - chip) * 2 + 1 - core

    def greet(self, barrier):
        for other in (self.sibling, self.far):
            pl.semaphore_signal(barrier, inc=1, device_id={"tp": other}, device_id_type=MESH)


def layer_kernel(
    count,
    q_hbm, k_hbm, v_hbm, res_hbm, w_hbm, gain_hbm, up_hbm, down_hbm, cg_hbm, src_hbm, cot_hbm,
    enc_ref, gq_ref, gk_ref, gv_ref, gres_ref,
    w, up, down, pick, cot, res, gain, cg_row, src_row,
    kbuf, vbuf, q, qwin, do, dwin, prob, probt, att, stat, swin, dcol, drow, twin,
    scaled, gcp, hid, actc, gcb, merged, gh, gacc, inv, unit, sigma, full1, full2,
    sb, rb, mine, s2b, r2b,
    load_sem, slab_sem, ks, kr, kf, vs, vr, vf, qs, qr, ts, tr, ds_, dr, es, er,
    s1, r1, s2, r2, ags, agr,
):
    blocks, group = Blocks(count), Group()
    groups, rows, width = sb.shape[2], s2b.shape[3], s2b.shape[4]
    half = groups * rows
    own = HALVES * rows
    heads = kbuf.shape[0]
    tok = HALVES * half
    src = up.shape[1]
    depth = src // PIECES

    def cols(cg):
        return pl.ds(pl.multiple_of(cg * width, width), width)

    def slab(owner):
        return pl.ds(pl.multiple_of(owner * rows, rows), rows)

    loads = {}

    def load(name, source, target, sem):
        loads.setdefault(name, []).append(pltpu.make_async_copy(source, target, sem))

    def arrived(name):
        for copy in loads[name]:
            copy.wait()

    for h in range(heads):
        span = pl.ds(h * HEAD_DIM, HEAD_DIM)
        load("k", k_hbm.at[:, span], kbuf.at[h, OWN], load_sem.at[2 * h])
        load("v", v_hbm.at[:, span], vbuf.at[h, OWN], load_sem.at[2 * h + 1])
    at = 2 * heads
    load("src", src_hbm, src_row, load_sem.at[at])
    load("cg", cg_hbm, cg_row, load_sem.at[at + 1])
    load("gain", gain_hbm, gain, load_sem.at[at + 2])
    load("w", w_hbm, w, load_sem.at[at + 3])
    load("up", up_hbm, up, load_sem.at[at + 4])
    load("res", res_hbm.at[pl.ds(pl.multiple_of(group.me * own, own), own)], res, load_sem.at[at + 5])
    at = at + 6
    for i in range(PIECES):
        span = pl.ds(i * depth, depth)
        load("down%d" % i, down_hbm.at[span], down.at[span], load_sem.at[at + i])
    for i in range(groups * HALVES):
        owner, h = divmod(i, HALVES)
        source = pl.ds(owner * own + h * rows, rows)
        load("cot", cot_hbm.at[source], cot.at[h, pl.ds(owner * rows, rows)], slab_sem.at[0, i])
        load("q", q_hbm.at[source], q.at[h, pl.ds(owner * rows, rows)], slab_sem.at[1, i])
    order = ["k", "v", "src", "cg", "q", "cot"] + ["down%d" % i for i in range(PIECES)]
    for name in order + ["gain", "w", "res", "up"]:
        for copy in loads[name]:
            copy.start()

    barrier = pltpu.get_barrier_semaphore()
    group.greet(barrier)
    blocks.greet(barrier)
    khalo = [Halo(blocks, kbuf.at[h], ks.at[h], kr.at[h], kf.at[h], True) for h in range(heads)]
    vhalo = [Halo(blocks, vbuf.at[h], vs.at[h], vr.at[h], vf.at[h], False) for h in range(heads)]
    arrived("k")
    arrived("v")
    blocks.greeted(barrier, 2)
    for h in range(heads):
        khalo[h].start()
        vhalo[h].start()

    def kslots(index):
        return kbuf.at[:, index]

    def vslots(index):
        return vbuf.at[:, index]

    blocks.clear(kslots)
    blocks.clear(vslots)
    for h in range(HALVES):
        blocks.clear(lambda index: qwin.at[h, index])
        blocks.clear(lambda index: dwin.at[h, index])
        blocks.clear(lambda index: twin.at[h, index])
    blocks.clear(lambda index: swin.at[index])

    arrived("src")
    arrived("cg")
    local = src_row[...] - group.me * src

    @pl.loop(0, PIECES)
    def _(i):
        place = lax.broadcasted_iota(jnp.int32, (depth, local.shape[1]), 0) + i * depth
        pick[pl.ds(pl.multiple_of(i * depth, depth), depth), :] = (
            jnp.where(place == local, 1.0, 0.0).astype(BF16)
        )

    ones = jnp.ones((16, local.shape[1]), BF16)
    inv[...] = 1.0 / (1.0 + dot_nt(ones, pick[...])[:8])

    def merged_grad(i):
        arrived("down%d" % i)
        span = slice(i * depth, (i + 1) * depth)
        for h in range(HALVES):
            scaled[h, :, span] = dot_nt(cot[h], down[span]) * inv[:1, span]

    stat_lane = lax.broadcasted_iota(jnp.int32, (tok, HEAD_DIM), 1)
    bias = jnp.concatenate(
        [
            jnp.full((1, tok), jnp.where(blocks.there(offset), 0.0, -1e30).astype(F32))
            for offset in OFFSETS
        ]
        + [jnp.zeros((1, tok), F32)],
        axis=1,
    )

    def attend(h, stats):
        khalo[h].arrive()
        vhalo[h].arrive()
        span = slice(h * HEAD_DIM, (h + 1) * HEAD_DIM)
        tops, inverses = [], []
        for part in range(HALVES):
            keys = kbuf[h].reshape(5 * tok, HEAD_DIM)
            scores = dot_nt(q[part, :, span], keys) * SCALE + bias
            top = jnp.max(scores, axis=1, keepdims=True)
            exps = jnp.exp(scores - top)
            inverse = 1.0 / jnp.sum(exps, axis=1, keepdims=True)
            low = (exps * inverse).astype(BF16)
            prob[h, part] = low
            att[part, :, span] = dot_nn(low, vbuf[h].reshape(5 * tok, HEAD_DIM)).astype(BF16)
            tops.append(top)
            inverses.append(inverse)
        stats = jnp.where(stat_lane == h, jnp.concatenate(tops, axis=0), stats)
        return jnp.where(stat_lane == heads + h, jnp.concatenate(inverses, axis=0), stats)

    def relay(h):
        khalo[h].relay()
        vhalo[h].relay()

    stats = jnp.zeros((tok, HEAD_DIM), F32)
    relay(0)
    arrived("cot")
    merged_grad(0)
    relay(1)
    merged_grad(1)
    arrived("q")
    stats = attend(0, stats)
    relay(2)
    merged_grad(2)
    merged_grad(3)
    stats = attend(1, stats)
    relay(3)
    for h in range(HALVES):
        gcp[h] = dot_nn(scaled[h].astype(BF16), pick[...]) * cg_row[...]
    for h in range(2, heads):
        stats = attend(h, stats)
    stat[...] = jnp.transpose(stats)[: 2 * heads]

    def qwindow(h):
        return lambda slot: qwin.at[h, slot]

    def dwindow(h):
        return lambda slot: dwin.at[h, slot]

    def twindow(h):
        return lambda slot: twin.at[h, slot]

    def swindow(slot):
        return swin.at[slot]

    def first(stage, h, cg):
        return remote(
            sb.at[stage, h, cg], rb.at[stage, h, cg], s1.at[stage, h, cg], r1.at[stage, h, cg],
            tp=group.sibling,
        )

    def second(stage, h, cg):
        return remote(
            s2b.at[stage, h, cg], r2b.at[stage, h, cg], s2.at[stage, h, cg], r2.at[stage, h, cg],
            tp=group.far,
        )

    def hop1(stage, h, cg, lhs_ref, product):
        lhs = jnp.concatenate(
            [
                lhs_ref[h, slab(o), :]
                for o in (group.across, group.sibling, group.far, group.me)
            ],
            axis=0,
        )
        part = product(lhs, cg).astype(BF16)
        sb[stage, h, cg] = part[: 2 * rows]
        mine[stage, h, cg] = part[2 * rows :]
        first(stage, h, cg).start()

    def hop2(stage, h, cg):
        first(stage, h, cg).wait_recv()
        s2b[stage, h, cg] = (
            mine[stage, h, cg, :rows].astype(F32) + rb[stage, h, cg, :rows].astype(F32)
        ).astype(BF16)
        second(stage, h, cg).start()

    def total(stage, h, cg):
        return (
            mine[stage, h, cg, rows:].astype(F32)
            + rb[stage, h, cg, rows:].astype(F32)
            + r2b[stage, h, cg].astype(F32)
        )

    def spread(stage, full, h, cg, kind):
        owner = group.far if kind == 2 else group.me
        to = group.far if kind == 0 else group.sibling
        ref = full.at[h, cg, slab(owner)]
        return remote(ref, ref, ags.at[stage, h, cg, kind], agr.at[stage, h, cg, kind], tp=to)

    def spread_own(stage, full, h):
        for cg in range(groups):
            spread(stage, full, h, cg, 0).start()
            spread(stage, full, h, cg, 1).start()

    def pass_on(stage, full, h, cg):
        spread(stage, full, h, cg, 0).wait_recv()
        spread(stage, full, h, cg, 2).start()

    def gather(stage, full, h, use):
        pass_on(stage, full, h, 0)

        @pl.loop(0, groups)
        def _(cg):
            @pl.when(cg + 1 < groups)
            def _():
                pass_on(stage, full, h, cg + 1)

            spread(stage, full, h, cg, 1).wait_recv()
            spread(stage, full, h, cg, 2).wait_recv()
            use(cg)

    def out_product(lhs, cg):
        return dot_nn(lhs, w[:, cols(cg)])

    def back_product(lhs, cg):
        return dot_nt(lhs, up[cols(cg), :])

    def ffn_product(lhs, cg):
        return dot_nn(lhs, down[:, cols(cg)])

    def reduce_all(stage, lhs_ref, product):
        for h in range(HALVES):
            @pl.loop(0, groups)
            def _(cg):
                hop1(stage, h, cg, lhs_ref, product)
                if h > 0:
                    hop2(stage, h - 1, cg)

        @pl.loop(0, groups)
        def _(cg):
            hop2(stage, HALVES - 1, cg)

    arrived("w")
    reduce_all(0, att, out_product)
    for h in range(HALVES):
        blocks.send(q.at[h], qwindow(h), qs.at[h], qr.at[h])
    blocks.send(stat, swindow, ts, tr)

    arrived("res")
    arrived("gain")
    scale = 1.0 / (groups * width)
    for h in range(HALVES):
        part = slice(h * rows, (h + 1) * rows)
        sums = jnp.zeros((rows, 1), F32)
        for cg in range(groups):
            second(0, h, cg).wait_recv()
            stream = res[part, cg * width : (cg + 1) * width].astype(F32) + total(0, h, cg)
            unit[h, cg] = stream
            sums = sums + jnp.sum(stream, axis=1, keepdims=True)
        mean = sums * scale
        squares = jnp.zeros((rows, 1), F32)
        for cg in range(groups):
            centered = unit[h, cg] - mean
            squares = squares + jnp.sum(centered * centered, axis=1, keepdims=True)
        deviation = jnp.sqrt(squares * scale + epsilon)
        sigma[h] = jnp.broadcast_to(deviation, (rows, HEAD_DIM))
        for cg in range(groups):
            level = (unit[h, cg] - mean) / deviation
            unit[h, cg] = level
            full1[h, cg, slab(group.me), :] = (
                level * gain[:, cg * width : (cg + 1) * width]
            ).astype(BF16)
        spread_own(0, full1, h)

    blocks.arrive(stat, swindow, ts, tr)
    for h in range(HALVES):
        blocks.arrive(q.at[h], qwindow(h), qs.at[h], qr.at[h])

    def row_of(ref, lead, line):
        return jnp.concatenate([lead(ref, slot)[line : line + 1, :] for slot in range(4)], axis=1)

    for part in range(HALVES):
        for h in range(heads):
            span = slice(h * HEAD_DIM, (h + 1) * HEAD_DIM)
            queries = qwin[part, :, :, span].reshape(4 * half, HEAD_DIM)
            lanes = slice(part * half, (part + 1) * half)
            top = jnp.concatenate([swin[s, h : h + 1, lanes] for s in range(4)], axis=1)
            inverse = jnp.concatenate(
                [swin[s, heads + h : heads + h + 1, lanes] for s in range(4)], axis=1
            )
            probt[h, part] = (
                jnp.exp(dot_nt(kbuf[h, OWN], queries) * SCALE - top) * inverse
            ).astype(BF16)

    arrived("up")
    tiles = src // TILE
    for h in range(HALVES):
        hid[h] = jnp.zeros(hid.shape[1:], F32)

        def use_hidden(cg):
            hid[h] += dot_nn(full1[h, cg], up[cols(cg), :])

        gather(0, full1, h, use_hidden)

        @pl.loop(0, tiles)
        def _(t):
            span = pl.ds(pl.multiple_of(t * TILE, TILE), TILE)
            copies = dot_nn(hid[h].astype(BF16), pick[:, span]) * cg_row[:, span]
            act, slope = gelu_slope(copies)
            actc[h, :, span] = act.astype(BF16)
            gcb[:, span] = (gcp[h, :, span] * slope).astype(BF16)

        @pl.loop(0, tiles)
        def _(t):
            span = pl.ds(pl.multiple_of(t * TILE, TILE), TILE)
            act, slope = gelu_slope(hid[h, :, span])
            hid[h, :, span] = act
            gh[h, :, span] = (
                scaled[h, :, span] * slope + dot_nt(gcb[...], pick[span, :])
            ).astype(BF16)

        @pl.loop(0, groups)
        def _(cg):
            hop1(1, h, cg, gh, back_product)

        @pl.loop(0, groups)
        def _(cg):
            hop2(1, h, cg)

    for h in range(HALVES):
        @pl.loop(0, tiles)
        def _(t):
            span = pl.ds(pl.multiple_of(t * TILE, TILE), TILE)
            merged[h, :, span] = (
                (hid[h, :, span] + dot_nt(actc[h], pick[span, :])) * inv[:1, span]
            ).astype(BF16)

        @pl.loop(0, groups)
        def _(cg):
            hop1(2, h, cg, merged, ffn_product)

    for h in range(HALVES):
        sums = jnp.zeros((rows, 1), F32)
        along = jnp.zeros((rows, 1), F32)
        pieces = []
        for cg in range(groups):
            span = slice(cg * width, (cg + 1) * width)
            second(1, h, cg).wait_recv()
            grad = cot[h, slab(group.me), span].astype(F32) + total(1, h, cg)
            graded = grad * gain[:, span]
            pieces.append(graded)
            sums = sums + jnp.sum(graded, axis=1, keepdims=True)
            along = along + jnp.sum(graded * unit[h, cg], axis=1, keepdims=True)
        for cg in range(groups):
            full2[h, cg, slab(group.me), :] = (
                (pieces[cg] - sums * scale - unit[h, cg] * (along * scale)) / sigma[h, :, :1]
            ).astype(BF16)
        spread_own(1, full2, h)

    for h in range(HALVES):
        @pl.loop(0, groups)
        def _(cg):
            hop2(2, h, cg)

    lane = lax.broadcasted_iota(jnp.int32, (half, HEAD_DIM), 1)

    def query_side(part):
        for h in range(heads):
            span = slice(h * HEAD_DIM, (h + 1) * HEAD_DIM)
            grads = do[part, :, span]
            chance = prob[h, part]
            slope = (
                chance.astype(F32)
                * (
                    dot_nt(grads, vbuf[h].reshape(5 * tok, HEAD_DIM))
                    - dcol[part, :, h : h + 1]
                )
            ).astype(BF16)
            gq_ref[part, :, span] = dot_nn(slope, kbuf[h].reshape(5 * tok, HEAD_DIM)) * SCALE
            near = slice(OWN * tok, (OWN + 1) * tok)
            grad_k = dot_tn(slope[:, near], q[part, :, span]) * SCALE
            grad_v = dot_tn(chance[:, near], grads)
            if part == 0:
                gk_ref[:, span] = grad_k
                gv_ref[:, span] = grad_v
            else:
                gk_ref[:, span] += grad_k
                gv_ref[:, span] += grad_v

    def key_side(part):
        blocks.arrive(do.at[part], dwindow(part), ds_.at[part], dr.at[part])
        blocks.arrive(drow.at[part], twindow(part), es.at[part], er.at[part])
        for h in range(heads):
            span = slice(h * HEAD_DIM, (h + 1) * HEAD_DIM)
            queries = qwin[part, :, :, span].reshape(4 * half, HEAD_DIM)
            grads = dwin[part, :, :, span].reshape(4 * half, HEAD_DIM)
            delta = jnp.concatenate([twin[part, s, h : h + 1, :] for s in range(4)], axis=1)
            chance = probt[h, part]
            slope = (chance.astype(F32) * (dot_nt(vbuf[h, OWN], grads) - delta)).astype(BF16)
            gv_ref[:, span] += dot_nn(chance, grads)
            gk_ref[:, span] += dot_nn(slope, queries) * SCALE

    for part in range(HALVES):
        gacc[...] = jnp.zeros(gacc.shape, F32)

        def use_low(cg):
            gacc[...] += dot_nt(full2[part, cg], w[:, cols(cg)])

        gather(1, full2, part, use_low)
        grad_att = gacc[...].astype(BF16)
        do[part] = grad_att
        blocks.send(do.at[part], dwindow(part), ds_.at[part], dr.at[part])
        deltas = jnp.zeros((half, HEAD_DIM), F32)
        for h in range(heads):
            span = slice(h * HEAD_DIM, (h + 1) * HEAD_DIM)
            delta = jnp.sum(
                grad_att[:, span].astype(F32) * att[part, :, span].astype(F32),
                axis=1, keepdims=True,
            )
            deltas = jnp.where(lane == h, delta, deltas)
        dcol[part] = deltas
        drow[part] = jnp.transpose(deltas)[:8]
        blocks.send(drow.at[part], twindow(part), es.at[part], er.at[part])
        gres_ref[part] = full2[part, group.me].astype(F32)
        query_side(part)
        if part < HALVES - 1:
            key_side(part)

    for h in range(HALVES):
        part = slice(h * rows, (h + 1) * rows)
        for cg in range(groups):
            span = slice(cg * width, (cg + 1) * width)
            second(2, h, cg).wait_recv()
            enc_ref[part, span] = unit[h, cg] * gain[:, span] + total(2, h, cg)
    key_side(HALVES - 1)

    for h in range(heads):
        khalo[h].left()
        vhalo[h].left()
    for h in range(HALVES):
        blocks.left(q.at[h], qwindow(h), qs.at[h], qr.at[h])
        blocks.left(do.at[h], dwindow(h), ds_.at[h], dr.at[h])
        blocks.left(drow.at[h], twindow(h), es.at[h], er.at[h])

        @pl.loop(0, groups)
        def _(cg):
            for stage in range(3):
                first(stage, h, cg).wait_send()
                second(stage, h, cg).wait_send()
            for kind in range(3):
                spread(0, full1, h, cg, kind).wait_send()
                spread(1, full2, h, cg, kind).wait_send()
    blocks.left(stat, swindow, ts, tr)


def layer(count, groups, q, k, v, res, w, gain, up, down, cg, source, cot):
    tok, head_cols = q.shape
    model = res.shape[1]
    heads = head_cols // HEAD_DIM
    src = up.shape[1]
    own = tok // groups
    rows, half, width = own // HALVES, tok // HALVES, model // groups
    copies = source.shape[1]
    dma = pltpu.SemaphoreType.DMA
    vm = pl.BlockSpec(memory_space=VM)
    far = pl.BlockSpec(memory_space=pl.ANY)
    grad = jax.ShapeDtypeStruct((tok, head_cols), F32)
    scratch = [
        VM(w.shape, BF16), VM(up.shape, BF16), VM(down.shape, BF16), VM((src, copies), BF16),
        VM((HALVES, half, model), BF16), VM((own, model), BF16),
        VM((1, model), F32), VM((1, copies), F32), VM((1, copies), jnp.int32),
        VM((heads, 5, tok, HEAD_DIM), BF16), VM((heads, 5, tok, HEAD_DIM), BF16),
        VM((HALVES, half, head_cols), BF16), VM((HALVES, 4, half, head_cols), BF16),
        VM((HALVES, half, head_cols), BF16), VM((HALVES, 4, half, head_cols), BF16),
        VM((heads, HALVES, half, 5 * tok), BF16), VM((heads, HALVES, tok, 4 * half), BF16),
        VM((HALVES, half, head_cols), BF16),
        VM((2 * heads, tok), F32), VM((4, 2 * heads, tok), F32),
        VM((HALVES, half, HEAD_DIM), F32), VM((HALVES, 8, half), F32), VM((HALVES, 4, 8, half), F32),
        VM((HALVES, half, src), F32), VM((HALVES, half, copies), F32), VM((HALVES, half, src), F32),
        VM((HALVES, half, copies), BF16), VM((half, copies), BF16),
        VM((HALVES, half, src), BF16), VM((HALVES, half, src), BF16), VM((half, head_cols), F32),
        VM((8, src), F32),
        VM((HALVES, groups, rows, width), F32), VM((HALVES, rows, HEAD_DIM), F32),
        VM((HALVES, groups, half, width), BF16), VM((HALVES, groups, half, width), BF16),
        VM((3, HALVES, groups, 2 * rows, width), BF16),
        VM((3, HALVES, groups, 2 * rows, width), BF16),
        VM((3, HALVES, groups, 2 * rows, width), BF16),
        VM((3, HALVES, groups, rows, width), BF16),
        VM((3, HALVES, groups, rows, width), BF16),
        dma((2 * heads + 6 + PIECES,)), dma((2, groups * HALVES)),
        dma((heads, 4)), dma((heads, 4)), dma((heads,)),
        dma((heads, 4)), dma((heads, 4)), dma((heads,)),
        dma((HALVES, 4)), dma((HALVES, 4)), dma((4,)), dma((4,)),
        dma((HALVES, 4)), dma((HALVES, 4)), dma((HALVES, 4)), dma((HALVES, 4)),
        dma((3, HALVES, groups)), dma((3, HALVES, groups)),
        dma((3, HALVES, groups)), dma((3, HALVES, groups)),
        dma((2, HALVES, groups, 3)), dma((2, HALVES, groups, 3)),
    ]
    return pl.pallas_call(
        functools.partial(layer_kernel, count),
        out_shape=(
            jax.ShapeDtypeStruct((own, model), F32),
            jax.ShapeDtypeStruct((HALVES, half, head_cols), F32),
            grad,
            grad,
            jax.ShapeDtypeStruct((HALVES, half, width), F32),
        ),
        in_specs=[far] * 11,
        out_specs=(vm,) * 5,
        scratch_shapes=scratch,
        compiler_params=pltpu.CompilerParams(
            collective_id=1, has_side_effects=True, vmem_limit_bytes=67043328
        ),
        name="layer",
    )(q, k, v, res, w, gain, up, down, cg, source, cot)


def emit_kernel(groups, enc, gq, gk, gv, gres, enc_out, gq_out, gk_out, gv_out, gres_out, sem):
    halves, half = gq.shape[:2]
    rows = half // groups
    own = halves * rows
    copies = [
        pltpu.make_async_copy(enc, enc_out, sem.at[0]),
        pltpu.make_async_copy(gk, gk_out, sem.at[1]),
        pltpu.make_async_copy(gv, gv_out, sem.at[2]),
    ]
    for i in range(groups * halves):
        owner, h = divmod(i, halves)
        there = pl.ds(owner * own + h * rows, rows)
        here = pl.ds(owner * rows, rows)
        copies.append(
            pltpu.make_async_copy(gq.at[h, here], gq_out.at[there], sem.at[3 + 2 * i])
        )
        copies.append(
            pltpu.make_async_copy(gres.at[h, here], gres_out.at[there], sem.at[4 + 2 * i])
        )
    for copy in copies:
        copy.start()
    for copy in copies:
        copy.wait()


def emit(groups, enc, gq, gk, gv, gres):
    halves, half, head_cols = gq.shape
    tok = halves * half
    grad = jax.ShapeDtypeStruct((tok, head_cols), F32)
    return pl.pallas_call(
        functools.partial(emit_kernel, groups),
        out_shape=(
            jax.ShapeDtypeStruct(enc.shape, F32), grad, grad, grad,
            jax.ShapeDtypeStruct((tok, gres.shape[2]), F32),
        ),
        in_specs=[pl.BlockSpec(memory_space=VM)] * 5,
        out_specs=(pl.BlockSpec(memory_space=pl.ANY),) * 5,
        scratch_shapes=[pltpu.SemaphoreType.DMA((3 + 2 * groups * halves,))],
        name="emit",
    )(enc, gq, gk, gv, gres)


def shards(
    count, groups, query_heads, key_heads, value_heads, residual, out_weight, ln_gain,
    up_source, down_source, copy_gain, neuron_source, cotangent,
):
    enc, gq, gk, gv, gres = layer(
        count, groups, query_heads, key_heads, value_heads, residual, out_weight,
        ln_gain[None, :], up_source, down_source, copy_gain[None, :], neuron_source[None, :],
        cotangent,
    )
    return emit(groups, enc, gq, gk, gv, gres)


def solution(mesh):
    in_specs = (
        P("seq", "tp"),
        P("seq", "tp"),
        P("seq", "tp"),
        P("seq", None),
        P("tp", None),
        P(),
        P(None, "tp"),
        P("tp", None),
        P("tp"),
        P("tp"),
        P("seq", None),
    )
    out_specs = (
        P(("seq", "tp"), None),
        P("seq", "tp"),
        P("seq", "tp"),
        P("seq", "tp"),
        P("seq", "tp"),
    )
    body = functools.partial(shards, mesh.shape["seq"], mesh.shape["tp"])
    return jax.shard_map(body, mesh=mesh, in_specs=in_specs, out_specs=out_specs, check_vma=False)
```

time: 145 us -> 116 us (0.80); the launches traced: 143 us -> 116 us
  Pallas kernels: 128 us -> 115 us
  local copies, waits for them, and re-layouts: 8.49 us -> 0 us
  other arithmetic: 5.55 us -> 0 us
    pallas_call x4 -> x2, Pallas kernels: 128 us -> 115 us  [the longest x1 111 us: layer(): pl.pallas_call(functools.partial(layer_kernel, count), out_shape=(jax.Sha...]
    unnamed x26 -> x0, local copies, waits for them, and re-layouts: 8.49 us -> none
    convert_element_type x2 -> x0, other arithmetic: 4.35 us -> none  [the longest x1 2.22 us: shards(): pick = pick.astype(BF16)]
where the time goes in v1:
time: 116 us
  Pallas kernels  115 us (99%)
    pallas_call x1, Pallas kernels, layer(): pl.pallas_call(functools.partial(layer_kernel, count), out_shape=(jax.Sha...  111 us
    pallas_call x1, Pallas kernels, emit(): pl.pallas_call(functools.partial(emit_kernel, groups), out_shape=(jax.Sha...  4 us

profile of v1, /device:TPU:0, one launch (start us, length us, event | category | flops | bytes accessed | tf_op | source)
XLA Modules:
  0.0 116.2 jit_solution(13272451026301550785)
XLA Ops:
  0.6 111.4 %layer.1 = (f32[64,4096]{1,0:T(8,128)}, f32[2,128,512]{2,1,0:T(8,128)}, f32[256,512]{1,0:T(8,128)}, f32[256,512]{1,0:T(8,128)}, f32[2,128,1024]{2,1,0:T(8,128)}) custom-call(bf16[256,512]{1,0:T(8,128)(2,1)} %q_hbm.1, bf16[256,512]{1,0:T(8,128)(2,1)} %k_hbm.1, bf16[256,512]{1,0:T(8,128)(2,1)} %v_hbm.1, bf16[256,4096]{1,0:T(8,128)(2,1)} %res_hbm.1, ...), custom_call_target="tpu_custom_call" | custom-call | tf_op jit(solution)/shard_map/layer/pallas_call | solution.py:716
  112.1 4.0 %emit.1 = (f32[64,4096]{1,0:T(8,128)}, f32[256,512]{1,0:T(8,128)}, f32[256,512]{1,0:T(8,128)}, f32[256,512]{1,0:T(8,128)}, f32[256,1024]{1,0:T(8,128)}) custom-call(f32[64,4096]{1,0:T(8,128)} %get-tuple-element.10.enc, f32[2,128,512]{2,1,0:T(8,128)} %get-tuple-element.11.gq, f32[256,512]{1,0:T(8,128)} %get-tuple-element.12.gk, ...), custom_call_target="tpu_custom_call" | custom-call | tf_op jit(solution)/shard_map/emit/pallas_call | solution.py:764

commit v2 on v1

--- a/solution.py
+++ b/solution.py
@@ -202,12 +202,12 @@
 def layer_kernel(
     count,
     q_hbm, k_hbm, v_hbm, res_hbm, w_hbm, gain_hbm, up_hbm, down_hbm, cg_hbm, src_hbm, cot_hbm,
-    enc_ref, gq_ref, gk_ref, gv_ref, gres_ref,
+    enc_ref, gq_ref, gk_ref, gv_ref, gres_ref, vown, qlast, dlast, tlast, plast,
     w, up, down, pick, cot, res, gain, cg_row, src_row,
     kbuf, vbuf, q, qwin, do, dwin, prob, probt, att, stat, swin, dcol, drow, twin,
-    scaled, gcp, hid, actc, gcb, merged, gh, gacc, inv, unit, sigma, full1, full2,
+    scaled, gcp, hid, actc, gcb, gh, gacc, inv, unit, sigma, full,
     sb, rb, mine, s2b, r2b,
-    load_sem, slab_sem, ks, kr, kf, vs, vr, vf, qs, qr, ts, tr, ds_, dr, es, er,
+    load_sem, slab_sem, cot_sem, ks, kr, kf, vs, vr, vf, qs, qr, ts, tr, ds_, dr, es, er,
     s1, r1, s2, r2, ags, agr,
 ):
     blocks, group = Blocks(count), Group()
@@ -245,17 +245,22 @@
     load("w", w_hbm, w, load_sem.at[at + 3])
     load("up", up_hbm, up, load_sem.at[at + 4])
     load("res", res_hbm.at[pl.ds(pl.multiple_of(group.me * own, own), own)], res, load_sem.at[at + 5])
-    at = at + 6
+    load("mine", cot_hbm.at[pl.ds(pl.multiple_of(group.me * own, own), own)], cot, load_sem.at[at + 6])
+    at = at + 7
     for i in range(PIECES):
         span = pl.ds(i * depth, depth)
         load("down%d" % i, down_hbm.at[span], down.at[span], load_sem.at[at + i])
     for i in range(groups * HALVES):
         owner, h = divmod(i, HALVES)
         source = pl.ds(owner * own + h * rows, rows)
-        load("cot", cot_hbm.at[source], cot.at[h, pl.ds(owner * rows, rows)], slab_sem.at[0, i])
-        load("q", q_hbm.at[source], q.at[h, pl.ds(owner * rows, rows)], slab_sem.at[1, i])
+        for cg in range(groups):
+            load(
+                "cot", cot_hbm.at[source, pl.ds(cg * width, width)],
+                full.at[h, cg, pl.ds(owner * rows, rows)], cot_sem.at[cg, i],
+            )
+        load("q", q_hbm.at[source], q.at[h, pl.ds(owner * rows, rows)], slab_sem.at[i])
     order = ["k", "v", "src", "cg", "q", "cot"] + ["down%d" % i for i in range(PIECES)]
-    for name in order + ["gain", "w", "res", "up"]:
+    for name in order + ["gain", "w", "res", "mine", "up"]:
         for copy in loads[name]:
             copy.start()
 
@@ -271,6 +276,20 @@
         khalo[h].start()
         vhalo[h].start()
 
+    last = HALVES - 1
+
+    def qwindow(h):
+        return lambda slot: qlast.at[slot] if h == last else qwin.at[h, slot]
+
+    def dwindow(h):
+        return lambda slot: dlast.at[slot] if h == last else dwin.at[h, slot]
+
+    def twindow(h):
+        return lambda slot: tlast.at[slot] if h == last else twin.at[h, slot]
+
+    def swindow(slot):
+        return swin.at[slot]
+
     def kslots(index):
         return kbuf.at[:, index]
 
@@ -280,9 +299,9 @@
     blocks.clear(kslots)
     blocks.clear(vslots)
     for h in range(HALVES):
-        blocks.clear(lambda index: qwin.at[h, index])
-        blocks.clear(lambda index: dwin.at[h, index])
-        blocks.clear(lambda index: twin.at[h, index])
+        blocks.clear(qwindow(h))
+        blocks.clear(dwindow(h))
+        blocks.clear(twindow(h))
     blocks.clear(lambda index: swin.at[index])
 
     arrived("src")
@@ -302,8 +321,13 @@
     def merged_grad(i):
         arrived("down%d" % i)
         span = slice(i * depth, (i + 1) * depth)
-        for h in range(HALVES):
-            scaled[h, :, span] = dot_nt(cot[h], down[span]) * inv[:1, span]
+        part = jnp.zeros((tok, depth), F32)
+        for cg in range(groups):
+            part = part + dot_nt(
+                full[:, cg].reshape(tok, width), down[span, cg * width : (cg + 1) * width]
+            )
+        part = part * inv[:1, span]
+        scaled[:, :, span] = part.astype(BF16).reshape(HALVES, half, depth)
 
     stat_lane = lax.broadcasted_iota(jnp.int32, (tok, HEAD_DIM), 1)
     bias = jnp.concatenate(
@@ -319,20 +343,17 @@
         khalo[h].arrive()
         vhalo[h].arrive()
         span = slice(h * HEAD_DIM, (h + 1) * HEAD_DIM)
-        tops, inverses = [], []
-        for part in range(HALVES):
-            keys = kbuf[h].reshape(5 * tok, HEAD_DIM)
-            scores = dot_nt(q[part, :, span], keys) * SCALE + bias
-            top = jnp.max(scores, axis=1, keepdims=True)
-            exps = jnp.exp(scores - top)
-            inverse = 1.0 / jnp.sum(exps, axis=1, keepdims=True)
-            low = (exps * inverse).astype(BF16)
-            prob[h, part] = low
-            att[part, :, span] = dot_nn(low, vbuf[h].reshape(5 * tok, HEAD_DIM)).astype(BF16)
-            tops.append(top)
-            inverses.append(inverse)
-        stats = jnp.where(stat_lane == h, jnp.concatenate(tops, axis=0), stats)
-        return jnp.where(stat_lane == heads + h, jnp.concatenate(inverses, axis=0), stats)
+        keys = kbuf[h].reshape(5 * tok, HEAD_DIM)
+        scores = dot_nt(q[:, :, span].reshape(tok, HEAD_DIM), keys) * SCALE + bias
+        top = jnp.max(scores, axis=1, keepdims=True)
+        exps = jnp.exp(scores - top)
+        inverse = 1.0 / jnp.sum(exps, axis=1, keepdims=True)
+        low = (exps * inverse).astype(BF16)
+        prob[h] = low.reshape(HALVES, half, 5 * tok)
+        out = dot_nn(low, vbuf[h].reshape(5 * tok, HEAD_DIM)).astype(BF16)
+        att[:, :, span] = out.reshape(HALVES, half, HEAD_DIM)
+        stats = jnp.where(stat_lane == h, top, stats)
+        return jnp.where(stat_lane == heads + h, inverse, stats)
 
     def relay(h):
         khalo[h].relay()
@@ -351,33 +372,22 @@
     merged_grad(3)
     stats = attend(1, stats)
     relay(3)
-    for h in range(HALVES):
-        gcp[h] = dot_nn(scaled[h].astype(BF16), pick[...]) * cg_row[...]
+    flat = scaled[...].reshape(tok, src)
+    gcp[...] = (dot_nn(flat, pick[...]) * cg_row[...]).astype(BF16).reshape(gcp.shape)
+    vown[...] = vbuf[:, OWN]
     for h in range(2, heads):
         stats = attend(h, stats)
     stat[...] = jnp.transpose(stats)[: 2 * heads]
 
-    def qwindow(h):
-        return lambda slot: qwin.at[h, slot]
-
-    def dwindow(h):
-        return lambda slot: dwin.at[h, slot]
-
-    def twindow(h):
-        return lambda slot: twin.at[h, slot]
-
-    def swindow(slot):
-        return swin.at[slot]
-
     def first(stage, h, cg):
         return remote(
-            sb.at[stage, h, cg], rb.at[stage, h, cg], s1.at[stage, h, cg], r1.at[stage, h, cg],
+            sb.at[stage % 2, h, cg], rb.at[stage % 2, h, cg], s1.at[stage, h, cg], r1.at[stage, h, cg],
             tp=group.sibling,
         )
 
     def second(stage, h, cg):
         return remote(
-            s2b.at[stage, h, cg], r2b.at[stage, h, cg], s2.at[stage, h, cg], r2.at[stage, h, cg],
+            s2b.at[stage % 2, h, cg], r2b.at[stage % 2, h, cg], s2.at[stage, h, cg], r2.at[stage, h, cg],
             tp=group.far,
         )
 
@@ -390,22 +400,22 @@
             axis=0,
         )
         part = product(lhs, cg).astype(BF16)
-        sb[stage, h, cg] = part[: 2 * rows]
-        mine[stage, h, cg] = part[2 * rows :]
+        sb[stage % 2, h, cg] = part[: 2 * rows]
+        mine[stage % 2, h, cg] = part[2 * rows :]
         first(stage, h, cg).start()
 
     def hop2(stage, h, cg):
         first(stage, h, cg).wait_recv()
-        s2b[stage, h, cg] = (
-            mine[stage, h, cg, :rows].astype(F32) + rb[stage, h, cg, :rows].astype(F32)
+        s2b[stage % 2, h, cg] = (
+            mine[stage % 2, h, cg, :rows].astype(F32) + rb[stage % 2, h, cg, :rows].astype(F32)
         ).astype(BF16)
         second(stage, h, cg).start()
 
     def total(stage, h, cg):
         return (
-            mine[stage, h, cg, rows:].astype(F32)
-            + rb[stage, h, cg, rows:].astype(F32)
-            + r2b[stage, h, cg].astype(F32)
+            mine[stage % 2, h, cg, rows:].astype(F32)
+            + rb[stage % 2, h, cg, rows:].astype(F32)
+            + r2b[stage % 2, h, cg].astype(F32)
         )
 
     def spread(stage, full, h, cg, kind):
@@ -484,30 +494,10 @@
         for cg in range(groups):
             level = (unit[h, cg] - mean) / deviation
             unit[h, cg] = level
-            full1[h, cg, slab(group.me), :] = (
+            full[h, cg, slab(group.me), :] = (
                 level * gain[:, cg * width : (cg + 1) * width]
             ).astype(BF16)
-        spread_own(0, full1, h)
-
-    blocks.arrive(stat, swindow, ts, tr)
-    for h in range(HALVES):
-        blocks.arrive(q.at[h], qwindow(h), qs.at[h], qr.at[h])
-
-    def row_of(ref, lead, line):
-        return jnp.concatenate([lead(ref, slot)[line : line + 1, :] for slot in range(4)], axis=1)
-
-    for part in range(HALVES):
-        for h in range(heads):
-            span = slice(h * HEAD_DIM, (h + 1) * HEAD_DIM)
-            queries = qwin[part, :, :, span].reshape(4 * half, HEAD_DIM)
-            lanes = slice(part * half, (part + 1) * half)
-            top = jnp.concatenate([swin[s, h : h + 1, lanes] for s in range(4)], axis=1)
-            inverse = jnp.concatenate(
-                [swin[s, heads + h : heads + h + 1, lanes] for s in range(4)], axis=1
-            )
-            probt[h, part] = (
-                jnp.exp(dot_nt(kbuf[h, OWN], queries) * SCALE - top) * inverse
-            ).astype(BF16)
+        spread_own(0, full, h)
 
     arrived("up")
     tiles = src // TILE
@@ -515,9 +505,9 @@
         hid[h] = jnp.zeros(hid.shape[1:], F32)
 
         def use_hidden(cg):
-            hid[h] += dot_nn(full1[h, cg], up[cols(cg), :])
-
-        gather(0, full1, h, use_hidden)
+            hid[h] += dot_nn(full[h, cg], up[cols(cg), :])
+
+        gather(0, full, h, use_hidden)
 
         @pl.loop(0, tiles)
         def _(t):
@@ -525,7 +515,7 @@
             copies = dot_nn(hid[h].astype(BF16), pick[:, span]) * cg_row[:, span]
             act, slope = gelu_slope(copies)
             actc[h, :, span] = act.astype(BF16)
-            gcb[:, span] = (gcp[h, :, span] * slope).astype(BF16)
+            gcb[:, span] = (gcp[h, :, span].astype(F32) * slope).astype(BF16)
 
         @pl.loop(0, tiles)
         def _(t):
@@ -533,29 +523,49 @@
             act, slope = gelu_slope(hid[h, :, span])
             hid[h, :, span] = act
             gh[h, :, span] = (
-                scaled[h, :, span] * slope + dot_nt(gcb[...], pick[span, :])
+                scaled[h, :, span].astype(F32) * slope + dot_nt(gcb[...], pick[span, :])
             ).astype(BF16)
 
         @pl.loop(0, groups)
         def _(cg):
+            for kind in range(3):
+                spread(0, full, h, cg, kind).wait_send()
             hop1(1, h, cg, gh, back_product)
 
         @pl.loop(0, groups)
         def _(cg):
             hop2(1, h, cg)
 
-    for h in range(HALVES):
+    def feed_forward():
         @pl.loop(0, tiles)
         def _(t):
             span = pl.ds(pl.multiple_of(t * TILE, TILE), TILE)
-            merged[h, :, span] = (
-                (hid[h, :, span] + dot_nt(actc[h], pick[span, :])) * inv[:1, span]
-            ).astype(BF16)
+            acts = hid[:, :, span].reshape(tok, TILE)
+            copied = dot_nt(actc[...].reshape(tok, actc.shape[2]), pick[span, :])
+            gh[:, :, span] = (
+                ((acts + copied) * inv[:1, span]).astype(BF16).reshape(HALVES, half, TILE)
+            )
+
+        for h in range(HALVES):
+            @pl.loop(0, groups)
+            def _(cg):
+                first(0, h, cg).wait_send()
+                second(0, h, cg).wait_send()
+
+        owners = (group.across, group.sibling, group.far, group.me)
 
         @pl.loop(0, groups)
         def _(cg):
-            hop1(2, h, cg, merged, ffn_product)
-
+            lhs = jnp.concatenate(
+                [gh[h, slab(o), :] for h in range(HALVES) for o in owners], axis=0
+            )
+            part = ffn_product(lhs, cg).astype(BF16)
+            for h in range(HALVES):
+                sb[0, h, cg] = part[h * half : h * half + 2 * rows]
+                mine[0, h, cg] = part[h * half + 2 * rows : (h + 1) * half]
+                first(2, h, cg).start()
+
+    arrived("mine")
     for h in range(HALVES):
         sums = jnp.zeros((rows, 1), F32)
         along = jnp.zeros((rows, 1), F32)
@@ -563,21 +573,43 @@
         for cg in range(groups):
             span = slice(cg * width, (cg + 1) * width)
             second(1, h, cg).wait_recv()
-            grad = cot[h, slab(group.me), span].astype(F32) + total(1, h, cg)
+            grad = cot[h * rows : (h + 1) * rows, span].astype(F32) + total(1, h, cg)
             graded = grad * gain[:, span]
             pieces.append(graded)
             sums = sums + jnp.sum(graded, axis=1, keepdims=True)
             along = along + jnp.sum(graded * unit[h, cg], axis=1, keepdims=True)
         for cg in range(groups):
-            full2[h, cg, slab(group.me), :] = (
+            full[h, cg, slab(group.me), :] = (
                 (pieces[cg] - sums * scale - unit[h, cg] * (along * scale)) / sigma[h, :, :1]
             ).astype(BF16)
-        spread_own(1, full2, h)
+        spread_own(1, full, h)
+        if h == 0:
+            feed_forward()
 
     for h in range(HALVES):
         @pl.loop(0, groups)
         def _(cg):
             hop2(2, h, cg)
+
+    blocks.arrive(stat, swindow, ts, tr)
+    for h in range(HALVES):
+        blocks.arrive(q.at[h], qwindow(h), qs.at[h], qr.at[h])
+
+    for part in range(HALVES):
+        for h in range(heads):
+            span = slice(h * HEAD_DIM, (h + 1) * HEAD_DIM)
+            window = qlast if part == last else qwin.at[part]
+            queries = window[:, :, span].reshape(4 * half, HEAD_DIM)
+            lanes = slice(part * half, (part + 1) * half)
+            top = jnp.concatenate([swin[s, h : h + 1, lanes] for s in range(4)], axis=1)
+            inverse = jnp.concatenate(
+                [swin[s, heads + h : heads + h + 1, lanes] for s in range(4)], axis=1
+            )
+            chance = jnp.exp(dot_nt(kbuf[h, OWN], queries) * SCALE - top) * inverse
+            if part == last:
+                plast[h] = chance.astype(BF16)
+            else:
+                probt[h, part] = chance.astype(BF16)
 
     lane = lax.broadcasted_iota(jnp.int32, (half, HEAD_DIM), 1)
 
@@ -604,9 +636,12 @@
                 gk_ref[:, span] += grad_k
                 gv_ref[:, span] += grad_v
 
-    def key_side(part):
+    def grads_arrive(part):
         blocks.arrive(do.at[part], dwindow(part), ds_.at[part], dr.at[part])
         blocks.arrive(drow.at[part], twindow(part), es.at[part], er.at[part])
+
+    def key_side(part):
+        grads_arrive(part)
         for h in range(heads):
             span = slice(h * HEAD_DIM, (h + 1) * HEAD_DIM)
             queries = qwin[part, :, :, span].reshape(4 * half, HEAD_DIM)
@@ -621,9 +656,9 @@
         gacc[...] = jnp.zeros(gacc.shape, F32)
 
         def use_low(cg):
-            gacc[...] += dot_nt(full2[part, cg], w[:, cols(cg)])
-
-        gather(1, full2, part, use_low)
+            gacc[...] += dot_nt(full[part, cg], w[:, cols(cg)])
+
+        gather(1, full, part, use_low)
         grad_att = gacc[...].astype(BF16)
         do[part] = grad_att
         blocks.send(do.at[part], dwindow(part), ds_.at[part], dr.at[part])
@@ -638,10 +673,11 @@
         dcol[part] = deltas
         drow[part] = jnp.transpose(deltas)[:8]
         blocks.send(drow.at[part], twindow(part), es.at[part], er.at[part])
-        gres_ref[part] = full2[part, group.me].astype(F32)
+        gres_ref[part] = full[part, group.me]
         query_side(part)
-        if part < HALVES - 1:
-            key_side(part)
+
+    for part in range(last):
+        key_side(part)
 
     for h in range(HALVES):
         part = slice(h * rows, (h + 1) * rows)
@@ -649,7 +685,7 @@
             span = slice(cg * width, (cg + 1) * width)
             second(2, h, cg).wait_recv()
             enc_ref[part, span] = unit[h, cg] * gain[:, span] + total(2, h, cg)
-    key_side(HALVES - 1)
+    grads_arrive(last)
 
     for h in range(heads):
         khalo[h].left()
@@ -661,12 +697,11 @@
 
         @pl.loop(0, groups)
         def _(cg):
-            for stage in range(3):
+            for stage in range(1, 3):
                 first(stage, h, cg).wait_send()
                 second(stage, h, cg).wait_send()
             for kind in range(3):
-                spread(0, full1, h, cg, kind).wait_send()
-                spread(1, full2, h, cg, kind).wait_send()
+                spread(1, full, h, cg, kind).wait_send()
     blocks.left(stat, swindow, ts, tr)
 
 
@@ -680,31 +715,31 @@
     copies = source.shape[1]
     dma = pltpu.SemaphoreType.DMA
     vm = pl.BlockSpec(memory_space=VM)
-    far = pl.BlockSpec(memory_space=pl.ANY)
+    far = pl.BlockSpec(memory_space=pltpu.HBM)
     grad = jax.ShapeDtypeStruct((tok, head_cols), F32)
     scratch = [
         VM(w.shape, BF16), VM(up.shape, BF16), VM(down.shape, BF16), VM((src, copies), BF16),
-        VM((HALVES, half, model), BF16), VM((own, model), BF16),
+        VM((own, model), BF16), VM((own, model), BF16),
         VM((1, model), F32), VM((1, copies), F32), VM((1, copies), jnp.int32),
         VM((heads, 5, tok, HEAD_DIM), BF16), VM((heads, 5, tok, HEAD_DIM), BF16),
-        VM((HALVES, half, head_cols), BF16), VM((HALVES, 4, half, head_cols), BF16),
-        VM((HALVES, half, head_cols), BF16), VM((HALVES, 4, half, head_cols), BF16),
-        VM((heads, HALVES, half, 5 * tok), BF16), VM((heads, HALVES, tok, 4 * half), BF16),
+        VM((HALVES, half, head_cols), BF16), VM((HALVES - 1, 4, half, head_cols), BF16),
+        VM((HALVES, half, head_cols), BF16), VM((HALVES - 1, 4, half, head_cols), BF16),
+        VM((heads, HALVES, half, 5 * tok), BF16), VM((heads, HALVES - 1, tok, 4 * half), BF16),
         VM((HALVES, half, head_cols), BF16),
         VM((2 * heads, tok), F32), VM((4, 2 * heads, tok), F32),
-        VM((HALVES, half, HEAD_DIM), F32), VM((HALVES, 8, half), F32), VM((HALVES, 4, 8, half), F32),
-        VM((HALVES, half, src), F32), VM((HALVES, half, copies), F32), VM((HALVES, half, src), F32),
+        VM((HALVES, half, HEAD_DIM), F32), VM((HALVES, 8, half), F32), VM((HALVES - 1, 4, 8, half), F32),
+        VM((HALVES, half, src), BF16), VM((HALVES, half, copies), BF16), VM((HALVES, half, src), F32),
         VM((HALVES, half, copies), BF16), VM((half, copies), BF16),
-        VM((HALVES, half, src), BF16), VM((HALVES, half, src), BF16), VM((half, head_cols), F32),
+        VM((HALVES, half, src), BF16), VM((half, head_cols), F32),
         VM((8, src), F32),
         VM((HALVES, groups, rows, width), F32), VM((HALVES, rows, HEAD_DIM), F32),
-        VM((HALVES, groups, half, width), BF16), VM((HALVES, groups, half, width), BF16),
-        VM((3, HALVES, groups, 2 * rows, width), BF16),
-        VM((3, HALVES, groups, 2 * rows, width), BF16),
-        VM((3, HALVES, groups, 2 * rows, width), BF16),
-        VM((3, HALVES, groups, rows, width), BF16),
-        VM((3, HALVES, groups, rows, width), BF16),
-        dma((2 * heads + 6 + PIECES,)), dma((2, groups * HALVES)),
+        VM((HALVES, groups, half, width), BF16),
+        VM((2, HALVES, groups, 2 * rows, width), BF16),
+        VM((2, HALVES, groups, 2 * rows, width), BF16),
+        VM((2, HALVES, groups, 2 * rows, width), BF16),
+        VM((2, HALVES, groups, rows, width), BF16),
+        VM((2, HALVES, groups, rows, width), BF16),
+        dma((2 * heads + 7 + PIECES,)), dma((groups * HALVES,)), dma((groups, groups * HALVES)),
         dma((heads, 4)), dma((heads, 4)), dma((heads,)),
         dma((heads, 4)), dma((heads, 4)), dma((heads,)),
         dma((HALVES, 4)), dma((HALVES, 4)), dma((4,)), dma((4,)),
@@ -720,46 +755,74 @@
             jax.ShapeDtypeStruct((HALVES, half, head_cols), F32),
             grad,
             grad,
-            jax.ShapeDtypeStruct((HALVES, half, width), F32),
+            jax.ShapeDtypeStruct((HALVES, half, width), BF16),
+            jax.ShapeDtypeStruct((heads, tok, HEAD_DIM), BF16),
+            jax.ShapeDtypeStruct((4, half, head_cols), BF16),
+            jax.ShapeDtypeStruct((4, half, head_cols), BF16),
+            jax.ShapeDtypeStruct((4, 8, half), F32),
+            jax.ShapeDtypeStruct((heads, tok, 4 * half), BF16),
         ),
         in_specs=[far] * 11,
-        out_specs=(vm,) * 5,
+        out_specs=(vm,) * 10,
         scratch_shapes=scratch,
         compiler_params=pltpu.CompilerParams(
-            collective_id=1, has_side_effects=True, vmem_limit_bytes=67043328
+            collective_id=1, has_side_effects=True, vmem_limit_bytes=50855936
         ),
         name="layer",
-    )(q, k, v, res, w, gain, up, down, cg, source, cot)
-
-
-def emit_kernel(groups, enc, gq, gk, gv, gres, enc_out, gq_out, gk_out, gv_out, gres_out, sem):
+    )(*[
+        pltpu.with_memory_space_constraint(x, pltpu.HBM)
+        for x in (q, k, v, res, w, gain, up, down, cg, source, cot)
+    ])
+
+
+def emit_kernel(
+    groups, enc, gq, gk, gv, gres, vown, qlast, dlast, tlast, plast,
+    enc_out, gq_out, gk_out, gv_out, gres_out, gk_sum, gv_sum, wide, sem, head_sem,
+):
     halves, half = gq.shape[:2]
     rows = half // groups
     own = halves * rows
-    copies = [
-        pltpu.make_async_copy(enc, enc_out, sem.at[0]),
-        pltpu.make_async_copy(gk, gk_out, sem.at[1]),
-        pltpu.make_async_copy(gv, gv_out, sem.at[2]),
-    ]
+    heads = vown.shape[0]
+    copies = [pltpu.make_async_copy(enc, enc_out, sem.at[0])]
+    copies[0].start()
+    wide[...] = gres[...].astype(F32)
     for i in range(groups * halves):
         owner, h = divmod(i, halves)
         there = pl.ds(owner * own + h * rows, rows)
         here = pl.ds(owner * rows, rows)
         copies.append(
-            pltpu.make_async_copy(gq.at[h, here], gq_out.at[there], sem.at[3 + 2 * i])
+            pltpu.make_async_copy(gq.at[h, here], gq_out.at[there], sem.at[1 + 2 * i])
         )
         copies.append(
-            pltpu.make_async_copy(gres.at[h, here], gres_out.at[there], sem.at[4 + 2 * i])
+            pltpu.make_async_copy(wide.at[h, here], gres_out.at[there], sem.at[2 + 2 * i])
         )
-    for copy in copies:
+    for copy in copies[1:]:
         copy.start()
+    for h in range(heads):
+        span = slice(h * HEAD_DIM, (h + 1) * HEAD_DIM)
+        queries = qlast[:, :, span].reshape(4 * half, HEAD_DIM)
+        grads = dlast[:, :, span].reshape(4 * half, HEAD_DIM)
+        delta = jnp.concatenate([tlast[s, h : h + 1, :] for s in range(4)], axis=1)
+        chance = plast[h]
+        slope = (chance.astype(F32) * (dot_nt(vown[h], grads) - delta)).astype(BF16)
+        gv_sum[h] = gv[:, span] + dot_nn(chance, grads)
+        gk_sum[h] = gk[:, span] + dot_nn(slope, queries) * SCALE
+        there = pl.ds(h * HEAD_DIM, HEAD_DIM)
+        outs = [
+            pltpu.make_async_copy(gv_sum.at[h], gv_out.at[:, there], head_sem.at[0, h]),
+            pltpu.make_async_copy(gk_sum.at[h], gk_out.at[:, there], head_sem.at[1, h]),
+        ]
+        for copy in outs:
+            copy.start()
+        copies += outs
     for copy in copies:
         copy.wait()
 
 
-def emit(groups, enc, gq, gk, gv, gres):
+def emit(groups, enc, gq, gk, gv, gres, vown, *rest):
     halves, half, head_cols = gq.shape
     tok = halves * half
+    heads = vown.shape[0]
     grad = jax.ShapeDtypeStruct((tok, head_cols), F32)
     return pl.pallas_call(
         functools.partial(emit_kernel, groups),
@@ -767,23 +830,30 @@
             jax.ShapeDtypeStruct(enc.shape, F32), grad, grad, grad,
             jax.ShapeDtypeStruct((tok, gres.shape[2]), F32),
         ),
-        in_specs=[pl.BlockSpec(memory_space=VM)] * 5,
+        in_specs=[pl.BlockSpec(memory_space=VM)] * 10,
         out_specs=(pl.BlockSpec(memory_space=pl.ANY),) * 5,
-        scratch_shapes=[pltpu.SemaphoreType.DMA((3 + 2 * groups * halves,))],
+        scratch_shapes=[
+            VM((heads, tok, HEAD_DIM), F32),
+            VM((heads, tok, HEAD_DIM), F32),
+            VM(gres.shape, F32),
+            pltpu.SemaphoreType.DMA((1 + 2 * groups * halves,)),
+            pltpu.SemaphoreType.DMA((2, heads)),
+        ],
+        compiler_params=pltpu.CompilerParams(vmem_limit_bytes=24 << 20),
         name="emit",
-    )(enc, gq, gk, gv, gres)
+    )(enc, gq, gk, gv, gres, vown, *rest)
 
 
 def shards(
     count, groups, query_heads, key_heads, value_heads, residual, out_weight, ln_gain,
     up_source, down_source, copy_gain, neuron_source, cotangent,
 ):
-    enc, gq, gk, gv, gres = layer(
+    parts = layer(
         count, groups, query_heads, key_heads, value_heads, residual, out_weight,
         ln_gain[None, :], up_source, down_source, copy_gain[None, :], neuron_source[None, :],
         cotangent,
     )
-    return emit(groups, enc, gq, gk, gv, gres)
+    return emit(groups, *parts)
 
 
 def solution(mesh):

time: 116 us -> 102 us (0.88)
  Pallas kernels: 115 us -> 101 us
    pallas_call x1, Pallas kernels: 111 us -> 98.5 us  [layer(): pl.pallas_call(functools.partial(layer_kernel, count), out_shape=(jax.Sha...]
    pallas_call x1, Pallas kernels: 4 us -> 2.49 us  [emit(): pl.pallas_call(functools.partial(emit_kernel, groups), out_shape=(jax.Sha...]
where the time goes in v2:
time: 102 us
  Pallas kernels  101 us (99%)
    pallas_call x1, Pallas kernels, layer(): pl.pallas_call(functools.partial(layer_kernel, count), out_shape=(jax.Sha...  98.5 us
    pallas_call x1, Pallas kernels, emit(): pl.pallas_call(functools.partial(emit_kernel, groups), out_shape=(jax.Sha...  2.49 us

profile of v2, /device:TPU:0, one launch (start us, length us, event | category | flops | bytes accessed | tf_op | source)
XLA Modules:
  0.0 101.8 jit_solution(9121930029488061685)
XLA Ops:
  0.6 98.5 %layer.1 = (f32[64,4096]{1,0:T(8,128)S(1)}, f32[2,128,512]{2,1,0:T(8,128)S(1)}, f32[256,512]{1,0:T(8,128)S(1)}, f32[256,512]{1,0:T(8,128)S(1)}, bf16[2,128,1024]...) custom-call(bf16[256,512]{1,0:T(8,128)(2,1)} %q_hbm.1, ...), custom_call_target="tpu_custom_call" | custom-call | tf_op jit(solution)/shard_map/layer/pallas_call | solution.py:751
  99.2 2.5 %emit.1 = (f32[64,4096]{1,0:T(8,128)}, f32[256,512]{1,0:T(8,128)}, f32[256,512]{1,0:T(8,128)}, f32[256,512]{1,0:T(8,128)}, f32[256,1024]{1,0:T(8,128)}) custom-call(f32[64,4096]{1,0:T(8,128)S(1)} %get-tuple-element.15.enc, f32[2,128,512]{2,1,0:T(8,128)S(1)} %get-tuple-element.16.gq, f32[256,512]{1,0:T(8,128)S(1)} %get-tuple-element.17.gk, ...), custom_call_target="tpu_custom_call" | custom-call | tf_op jit(solution)/shard_map/emit/pallas_call | solution.py:827

commit v3 on v2

--- a/solution.py
+++ b/solution.py
@@ -532,9 +532,11 @@
                 spread(0, full, h, cg, kind).wait_send()
             hop1(1, h, cg, gh, back_product)
 
-        @pl.loop(0, groups)
-        def _(cg):
-            hop2(1, h, cg)
+            @pl.when(cg > 0)
+            def _():
+                hop2(1, h, cg - 1)
+
+        hop2(1, h, groups - 1)
 
     def feed_forward():
         @pl.loop(0, tiles)

time: 102 us -> 101 us (level)
  Pallas kernels: 101 us -> 99.8 us
    pallas_call x1, Pallas kernels: 98.5 us -> 97.3 us  [layer(): pl.pallas_call(functools.partial(layer_kernel, count), out_shape=(jax.Sha...]
where the time goes in v3:
time: 101 us
  Pallas kernels  99.8 us (99%)
    pallas_call x1, Pallas kernels, layer(): pl.pallas_call(functools.partial(layer_kernel, count), out_shape=(jax.Sha...  97.3 us
    pallas_call x1, Pallas kernels, emit(): pl.pallas_call(functools.partial(emit_kernel, groups), out_shape=(jax.Sha...  2.49 us

profile of v3, /device:TPU:0, one launch (start us, length us, event | category | flops | bytes accessed | tf_op | source)
XLA Modules:
  0.0 100.6 jit_solution(17542373379215034357)
XLA Ops:
  0.6 97.3 %layer.1 = (f32[64,4096]{1,0:T(8,128)S(1)}, f32[2,128,512]{2,1,0:T(8,128)S(1)}, f32[256,512]{1,0:T(8,128)S(1)}, f32[256,512]{1,0:T(8,128)S(1)}, bf16[2,128,1024]...) custom-call(bf16[256,512]{1,0:T(8,128)(2,1)} %q_hbm.1, ...), custom_call_target="tpu_custom_call" | custom-call | tf_op jit(solution)/shard_map/layer/pallas_call | solution.py:753
  98.0 2.5 %emit.1 = (f32[64,4096]{1,0:T(8,128)}, f32[256,512]{1,0:T(8,128)}, f32[256,512]{1,0:T(8,128)}, f32[256,512]{1,0:T(8,128)}, f32[256,1024]{1,0:T(8,128)}) custom-call(f32[64,4096]{1,0:T(8,128)S(1)} %get-tuple-element.15.enc, f32[2,128,512]{2,1,0:T(8,128)S(1)} %get-tuple-element.16.gq, f32[256,512]{1,0:T(8,128)S(1)} %get-tuple-element.17.gk, ...), custom_call_target="tpu_custom_call" | custom-call | tf_op jit(solution)/shard_map/emit/pallas_call | solution.py:829
